TPU v7x, 32 devices: a whole 2x2x4 slice. The times are simulated.
32 devices in a mesh: groups: 2 (over x), slab: 16 (over z, y, core).
Axes of the slice: x: 2, y: 2, z: 4, core: 2. Of those that a mesh axis runs over, the one named last changes fastest.
Arguments:
- wave_now: float32 [4, 16, 32, 8, 1024], P('groups', 'slab'), parts along dimension 0, may hold values from -6 to 6
- wave_prev: float32 [4, 16, 32, 8, 1024], P('groups', 'slab'), parts along dimension 0, may hold values from -6 to 6
- potential: float32 [16, 32, 8, 1024], P('slab'), may hold values from -1.5 to 1.5
- angular_dvr: float32 [1024, 1024], replicated, may hold values from -0.1875 to 0.1875
- kinetic_radial: float32 [16, 16], replicated, may hold values from -1.5 to 1.5
- kinetic_bond: float32 [32, 32], replicated, may hold values from -1 to 1
- kinetic_third: float32 [8, 8], replicated, may hold values from -2 to 2
- inv_moment: float32 [16], P('slab'), may hold values from 0.2 to 2
- rot_level: float32 [1024], replicated, may hold values from 0.1 to 2
- helicity: float32 [2], replicated, may hold values from 0 to 1.5
- coriolis: float32 [1], replicated, may hold values from 0.5 to 1.5
- ladder: float32 [1024], replicated, may hold values from 0.2 to 1.5
- damping: float32 [16, 32, 8], P('slab'), may hold values from 0.5 to 1
- strip_bond: int32 [16, 128], P('slab'), may hold values from 0 to 28
- strip_third: int32 [16, 128], P('slab'), may hold values from 0 to 7
- strip_weight: float32 [16, 128, 4], P('slab'), may hold values from -3 to 3
- strip_length: int32 [16], P('slab'), may hold values from 1 to 128, 1843 in all
- strip_owner: int32 [16, 128, 1], P('slab'), may hold values from 0 to 15; in each aligned block of 128 rows (0 to 127, 128 to 255, ..., all dimensions but the last counted through in order) at most 16 rows name the same one
- strip_cell: int32 [16, 128], P('slab'), may hold values from 0 to 63
Outputs:
- wave_next: float32 [4, 16, 32, 8, 1024], P('groups', 'slab'), parts along dimension 0
- surface_flux: float32 [4, 1024, 1024], P('groups', 'slab'), parts along dimension 0
There are 2 independent parts, one for each index of `groups`. A program takes and returns all parts, laid end to end along the dimension named above; an argument that names none is the same for every part. Nothing has to cross between parts.
Inputs may be any that keep to these rules, and one draw needn't show every extreme that they name: `strip_owner`: among the 128 points of one R index, at most 16 name the same owner, and in every draw some owner is named by exactly 16 of them. `strip_length`: some R index has all 128 points live in every draw.
All inputs are finite; a program needn't handle non-finite values. No bound on the sum of `strip_length` on one device may be relied on, other than what follows from the above.
Results may differ from a plain program's by a relative error of at most 0.0003.
Values sent between devices are 32-bit elements; how exact they have to be, the bound alone decides.
A program may use at most 128 MiB of HBM per device.

v0:
```python
import jax
import jax.numpy as jnp
from jax import lax
from jax.sharding import PartitionSpec as P

SMAX = 128
P_DEV = 64


exact_prec = lax.Precision.HIGHEST


def hamiltonian_apply(
    wave,
    radial_term,
    potential,
    angular_dvr,
    kinetic_bond,
    kinetic_third,
    inv_moment,
    rot_level,
    helicity,
    coriolis,
    ladder,
):
    bond_term = jnp.einsum("ij,kqjza->kqiza", kinetic_bond, wave, precision=exact_prec)
    third_term = jnp.einsum("ij,kqrja->kqria", kinetic_third, wave, precision=exact_prec)
    grid_wave = jnp.einsum("kqrzb,ba->kqrza", wave, angular_dvr, precision=exact_prec)
    potential_term = jnp.einsum(
        "kqrza,ba->kqrzb", potential[None] * grid_wave, angular_dvr, precision=exact_prec
    )
    moment = inv_moment[None, :, None, None, None]
    rotation_term = (
        moment * (rot_level[None, None, None, None, :] + helicity[:, None, None, None, None]) * wave
    )
    padding = jnp.zeros((1,) + wave.shape[1:], jnp.float32)
    couple = coriolis[:, None, None, None, None]
    above = jnp.concatenate([wave[1:] * couple, padding], axis=0)
    below = jnp.concatenate([padding, wave[:-1] * couple], axis=0)
    coriolis_term = moment * ladder[None, None, None, None, :] * (above + below)
    return radial_term + bond_term + third_term + potential_term + rotation_term + coriolis_term


def local(
    wave_now,
    wave_prev,
    potential,
    angular_dvr,
    kinetic_radial,
    kinetic_bond,
    kinetic_third,
    inv_moment,
    rot_level,
    helicity,
    coriolis,
    ladder,
    damping,
    strip_bond,
    strip_third,
    strip_weight,
    strip_length,
    strip_owner,
    strip_cell,
):
    blocks, local_rows, bond_pts, thirds, angles = wave_now.shape
    flat_wave = wave_now.reshape(blocks, local_rows, bond_pts * thirds, angles)
    mixed = jnp.einsum(
        "ij,kjca->kica",
        kinetic_radial,
        lax.all_to_all(flat_wave, "slab", split_axis=2, concat_axis=1, tiled=True),
        precision=exact_prec,
    )
    radial_term = lax.all_to_all(mixed, "slab", split_axis=1, concat_axis=2, tiled=True).reshape(
        wave_now.shape
    )
    devices = lax.axis_size("slab")
    slot_count = max(2, 2 * SMAX // devices)
    points = local_rows * SMAX
    cells = wave_now.reshape(blocks, local_rows * bond_pts * thirds, angles)
    stencil_step = jnp.arange(4, dtype=jnp.int32)
    offset = jnp.arange(local_rows, dtype=jnp.int32)[:, None, None] * (bond_pts * thirds)
    cell_idx = (
        offset
        + (strip_bond[:, :, None] + stencil_step[None, None, :]) * thirds
        + strip_third[:, :, None]
    )
    stencil = jnp.take(cells, cell_idx.reshape(-1), axis=1).reshape(blocks, points, 4, angles)
    weights = strip_weight.reshape(points, 4)
    surface = jnp.einsum("pt,kpta->kpa", weights, stencil, precision=exact_prec)
    alive_mask = (
        (jnp.arange(SMAX, dtype=jnp.int32)[None, :] < strip_length[:, None])
        .reshape(points)
        .astype(jnp.float32)
    )
    surface = surface * alive_mask[None, :, None]
    owner = strip_owner.reshape(points)
    onehot = (owner[:, None] == jnp.arange(devices, dtype=jnp.int32)[None, :]).astype(jnp.float32)
    point_iota = jnp.arange(points, dtype=jnp.int32)
    earlier = (point_iota[None, :] < point_iota[:, None]).astype(jnp.float32)
    before = jnp.dot(earlier, onehot, precision=exact_prec)
    order_in = jnp.sum(onehot * before, axis=1).astype(jnp.int32)
    slot_idx = owner * slot_count + order_in
    select = (
        slot_idx[None, :] == jnp.arange(devices * slot_count, dtype=jnp.int32)[:, None]
    ).astype(jnp.float32)
    values = jnp.einsum("qp,kpa->qka", select, surface, precision=exact_prec).reshape(
        devices, slot_count, blocks, angles
    )
    cell_ids = jnp.dot(
        select, strip_cell.reshape(points).astype(jnp.float32), precision=exact_prec
    ).reshape(devices, slot_count)
    got_values, got_cells = (
        lax.all_to_all(values, "slab", split_axis=0, concat_axis=0, tiled=True),
        lax.all_to_all(cell_ids, "slab", split_axis=0, concat_axis=0, tiled=True),
    )
    landing = (
        got_cells.reshape(-1)[None, :] == jnp.arange(P_DEV, dtype=jnp.float32)[:, None]
    ).astype(jnp.float32)
    surface_flux = jnp.einsum(
        "cq,qka->kca",
        landing,
        got_values.reshape(devices * slot_count, blocks, angles),
        precision=exact_prec,
    )
    hamiltonian = hamiltonian_apply(
        wave_now,
        radial_term,
        potential,
        angular_dvr,
        kinetic_bond,
        kinetic_third,
        inv_moment,
        rot_level,
        helicity,
        coriolis,
        ladder,
    )
    damp = damping[None, :, :, :, None]
    wave_next = damp * (0.5 * hamiltonian - damp * wave_prev)
    return (wave_next, surface_flux)


def solution(mesh):
    in_specs = (
        P("groups", "slab", None, None, None),
        P("groups", "slab", None, None, None),
        P("slab", None, None, None),
        P(),
        P(),
        P(),
        P(),
        P("slab"),
        P(),
        P(),
        P(),
        P(),
        P("slab", None, None),
        P("slab", None),
        P("slab", None),
        P("slab", None, None),
        P("slab"),
        P("slab", None, None),
        P("slab", None),
    )
    out_specs = (P("groups", "slab", None, None, None), P("groups", "slab", None))
    return jax.shard_map(local, mesh=mesh, in_specs=in_specs, out_specs=out_specs, check_vma=False)
```

profile of v0, /device:TPU:13, one launch (start us, length us, event | category | flops | bytes accessed | tf_op | source)
XLA Modules:
  0.0 189.6 jit_solution(16299461356161265309)
XLA Ops:
  2.2 1.9 convolution_bitcast_fusion.1
  4.1 6.5 %all-to-all-start.3 = ((f32[16,1,16]{2,1,0:T(1,128)}), f32[16,1,16]{2,1,0:T(1,128)S(1)}, u32[]{:S(2)}, u32[]{:S(2)}) async-start(f32[16,1,16]{2,1,0:T(1,128)} %convolution_bitcast_fusion.1), calls=%async_computation.3 | async-start | bytes 16384 | tf_op jit(solution)/shard_map/all_to_all | solution.py:114
  10.6 4.6 %copy.58 = f32[2,1,32,8,1024]{4,0,3,2,1:T(2,128)} copy(f32[2,1,32,8,1024]{4,3,2,1,0:T(8,128)} %param.19) | data formatting | bytes 4194304 | tf_op args[0]
  15.3 6.5 %all-to-all-start = ((f32[2,1,256,1024]{3,0,1,2:T(2,128)}), f32[2,1,256,1024]{3,0,1,2:T(2,128)S(1)}, u32[]{:S(2)}, u32[]{:S(2)}) async-start(f32[2,1,256,1024]{3,0,1,2:T(2,128)} %bitcast.1), calls=%async_computation | async-start | bytes 4194304 | tf_op jit(solution)/shard_map/all_to_all | solution.py:70
  23.3 21.3 %gather_fusion = f32[512,2,1024]{2,1,0:T(2,128)} fusion(f32[2,256,1024]{2,0,1:T(2,128)} %bitcast.26, s32[1024]{0:T(1024)S(1)} %pad_clamp_fusion), kind=kCustom, calls=%fused_computation | custom fusion | bytes 8390656 | tf_op jit(solution)/shard_map/jit(_take)/gather | solution.py:87
  44.6 4.2 %broadcast_select_fusion = f32[2,128,4,1024]{3,0,2,1:T(2,128)S(1)} fusion(f32[2,128,4,1024]{3,0,2,1:T(2,128)} %bitcast.114, pred[128,4]{1,0:T(8,128)(4,1)S(1)} %copy.71), kind=kLoop, calls=%fused_computation.7 | loop fusion | flops 1048576 | bytes 8389120 | tf_op jit(solution)/shard_map/jit(_take)/select_n | solution.py:87
  48.8 8.4 %fusion.4 = f32[128,1,2,1024]{3,1,2,0:T(1,128)S(1)} fusion(f32[128,4,1,1]{1,2,3,0:T(1,128)S(1)} %copy.83, f32[2,128,4,1024]{3,0,2,1:T(2,128)S(1)} %broadcast_select_fusion), kind=kOutput, calls=%fused_computation.5 | convolution fusion | flops 12582912 | bytes 5244928 | tf_op jit(solution)/shard_map/pt,kpta->kpa/dot_general | solution.py:89
  58.5 1.5 copy.73
  60.0 9.1 %all-to-all-done = f32[2,1,256,1024]{3,0,1,2:T(2,128)S(1)} async-done(((f32[2,1,256,1024]{3,0,1,2:T(2,128)}), f32[2,1,256,1024]{3,0,1,2:T(2,128)S(1)}, u32[]{:S(2)}, u32[]{:S(2)}) %all-to-all-start) | async-done | bytes 2097184 | tf_op jit(solution)/shard_map/all_to_all | solution.py:70
  69.1 4.8 %all-to-all-start.2 = ((f32[16,16,2,1024]{3,1,2,0:T(8,128)}), f32[16,16,2,1024]{3,1,2,0:T(8,128)}, u32[]{:S(2)}, u32[]{:S(2)}) async-start(f32[16,16,2,1024]{3,1,2,0:T(8,128)} %copy.73), calls=%async_computation.2 | async-start | bytes 4194304 | tf_op jit(solution)/shard_map/all_to_all | solution.py:113
  73.9 3.4 %fusion.19 = f32[2,16,16,1024]{3,1,2,0:T(8,128)S(1)} fusion(f32[2,16,16,1024]{3,0,2,1:T(2,128)S(1)} %bitcast.113, f32[16,16]{1,0:T(8,128)S(1)} %copy-done.7), kind=kOutput, calls=%fused_computation.22 | convolution fusion | flops 100663296 | bytes 4195328 | tf_op jit(solution)/shard_map/ij,kjca->kica/dot_general | solution.py:67
  77.3 2.5 %copy.61 = f32[2,16,16,1024]{3,2,0,1:T(8,128)} copy(f32[2,16,16,1024]{3,1,2,0:T(8,128)S(1)} %fusion.19) | data formatting | bytes 4194304 | tf_op jit(solution)/shard_map/ij,kjca->kica/transpose | solution.py:67
  79.8 41.6 %all-to-all-done.2 = f32[16,16,2,1024]{3,1,2,0:T(8,128)} async-done(((f32[16,16,2,1024]{3,1,2,0:T(8,128)}), f32[16,16,2,1024]{3,1,2,0:T(8,128)}, u32[]{:S(2)}, u32[]{:S(2)}) %all-to-all-start.2) | async-done | bytes 2097184 | tf_op jit(solution)/shard_map/all_to_all | solution.py:113
  121.4 4.9 %all-to-all-start.1 = ((f32[2,16,16,1024]{3,2,0,1:T(8,128)}), f32[2,16,16,1024]{3,2,0,1:T(8,128)}, u32[]{:S(2)}, u32[]{:S(2)}) async-start(f32[2,16,16,1024]{3,2,0,1:T(8,128)} %copy.61), calls=%async_computation.1 | async-start | bytes 4194304 | tf_op jit(solution)/shard_map/all_to_all | solution.py:73
  129.0 1.3 slice_multiply_fusion.1
  130.3 3.4 %fusion.41 = f32[2,32,1024,8]{2,3,1,0:T(8,128)} fusion(f32[8,8]{1,0:T(8,128)S(1)} %copy-done.8, f32[2,1,32,8,1024]{4,3,2,1,0:T(8,128)S(1)} %copy-done.1), kind=kOutput, calls=%fused_computation.53 | convolution fusion | flops 50331648 | bytes 4194560 | tf_op jit(solution)/shard_map/ij,kqrja->kqria/dot_general | solution.py:27
  133.7 7.0 %fusion.22 = f32[2,32,8,1024]{3,2,1,0:T(8,128)S(1)} fusion(f32[1024,1024]{1,0:T(8,128)S(1)} %copy-done.2, f32[32,8,1024]{2,1,0:T(8,128)S(1)} %bitcast.118, f32[2,1,32,8,1024]{4,3,2,1,0:T(8,128)S(1)} %copy-done.1), kind=kOutput, calls=%fused_computation.23 | convolution fusion | flops 6442975232 | bytes 9437184 | tf_op jit(solution)/shard_map/kqrzb,ba->kqrza/dot_general | solution.py:28
  140.7 9.4 %fusion = f32[2,32,8,1024]{3,1,2,0:T(8,128)} fusion(f32[1024,1024]{1,0:T(8,128)S(1)} %copy-done.2, f32[2,32,8,1024]{3,2,1,0:T(8,128)S(1)} %fusion.22), kind=kOutput, calls=%fused_computation.1 | convolution fusion | flops 6442450944 | bytes 8388608 | tf_op jit(solution)/shard_map/kqrza,ba->kqrzb/dot_general | solution.py:29
  151.4 1.7 copy.74
  153.1 1.7 convolution_bitcast_fusion
  154.8 18.9 %all-to-all-done.1 = f32[2,16,16,1024]{3,2,0,1:T(8,128)} async-done(((f32[2,16,16,1024]{3,2,0,1:T(8,128)}), f32[2,16,16,1024]{3,2,0,1:T(8,128)}, u32[]{:S(2)}, u32[]{:S(2)}) %all-to-all-start.1) | async-done | bytes 2097184 | tf_op jit(solution)/shard_map/all_to_all | solution.py:73
  173.7 1.9 copy.62
  176.6 10.2 %fusion.11 = f32[2,1,32,8,1024]{4,2,3,0,1:T(8,128)S(1)} fusion(f32[2,32,8,1024]{3,1,2,0:T(8,128)S(1)} %copy-done.4, f32[2,1,32,8,1024]{4,3,2,1,0:T(8,128)} %param.20, f32[2,32,1024,8]{2,3,1,0:T(8,128)S(1)} %copy-done.3, f32[2,1,32,8,1024]{4,3,2,0,1:T(8,128)S(1)} %bitcast.115, f32[1,1,32,8,1024]{4,2,3,0,1:T(8,128)} %get-tuple-element.11, ...), kind=kOutput, calls=%fused_computation.14 | convolution fusion | flops 207618048 | bytes 16794624 | tf_op jit(solution)/shard_map/ij,kqjza->kqiza/dot_general | solution.py:26
  186.8 2.5 %copy.75 = f32[2,1,32,8,1024]{4,3,2,1,0:T(8,128)} copy(f32[2,1,32,8,1024]{4,2,3,0,1:T(8,128)S(1)} %fusion.11) | data formatting | bytes 4194304
  (53 shorter events, 7.2 us)
Async XLA Ops:
  0.6 175.0 %copy-start = (f32[32,32]{1,0:T(8,128)S(1)}, f32[32,32]{1,0:T(8,128)}, u32[]{:S(2)}) copy-start(f32[32,32]{1,0:T(8,128)} %param.24) | copy-start | bytes 12292
  4.1 11.1 %all-to-all-start.3 = ((f32[16,1,16]{2,1,0:T(1,128)}), f32[16,1,16]{2,1,0:T(1,128)S(1)}, u32[]{:S(2)}, u32[]{:S(2)}) async-start(f32[16,1,16]{2,1,0:T(1,128)} %convolution_bitcast_fusion.1), calls=%async_computation.3 | async-start | bytes 16384 | tf_op jit(solution)/shard_map/all_to_all | solution.py:114
  15.2 6.6 %copy-start.13 = (s32[1,128]{1,0:T(1,128)S(1)}, s32[1,128]{1,0:T(1,128)}, u32[]{:S(2)}) copy-start(s32[1,128]{1,0:T(1,128)} %param.32) | copy-start | bytes 1540
  15.2 6.8 %copy-start.12 = (s32[1,128]{1,0:T(1,128)S(1)}, s32[1,128]{1,0:T(1,128)}, u32[]{:S(2)}) copy-start(s32[1,128]{1,0:T(1,128)} %param.33) | copy-start | bytes 1540
  15.3 7.2 %copy-start.11 = (f32[1,128,4]{1,2,0:T(4,128)S(1)}, f32[1,128,4]{1,2,0:T(4,128)}, u32[]{:S(2)}) copy-start(f32[1,128,4]{1,2,0:T(4,128)} %param.34) | copy-start | bytes 6148
  15.3 53.9 %all-to-all-start = ((f32[2,1,256,1024]{3,0,1,2:T(2,128)}), f32[2,1,256,1024]{3,0,1,2:T(2,128)S(1)}, u32[]{:S(2)}, u32[]{:S(2)}) async-start(f32[2,1,256,1024]{3,0,1,2:T(2,128)} %bitcast.1), calls=%async_computation | async-start | bytes 4194304 | tf_op jit(solution)/shard_map/all_to_all | solution.py:70
  60.0 13.9 %copy-start.7 = (f32[16,16]{1,0:T(8,128)S(1)}, f32[16,16]{1,0:T(8,128)}, u32[]{:S(2)}) copy-start(f32[16,16]{1,0:T(8,128)} %param.23) | copy-start | bytes 3076
  69.1 52.3 %all-to-all-start.2 = ((f32[16,16,2,1024]{3,1,2,0:T(8,128)}), f32[16,16,2,1024]{3,1,2,0:T(8,128)}, u32[]{:S(2)}, u32[]{:S(2)}) async-start(f32[16,16,2,1024]{3,1,2,0:T(8,128)} %copy.73), calls=%async_computation.2 | async-start | bytes 4194304 | tf_op jit(solution)/shard_map/all_to_all | solution.py:113
  79.8 46.6 %copy-start.1 = (f32[2,1,32,8,1024]{4,3,2,1,0:T(8,128)S(1)}, f32[2,1,32,8,1024]{4,3,2,1,0:T(8,128)}, u32[]{:S(2)}) copy-start(f32[2,1,32,8,1024]{4,3,2,1,0:T(8,128)} %param.19) | copy-start | bytes 6291460
  121.4 52.3 %all-to-all-start.1 = ((f32[2,16,16,1024]{3,2,0,1:T(8,128)}), f32[2,16,16,1024]{3,2,0,1:T(8,128)}, u32[]{:S(2)}, u32[]{:S(2)}) async-start(f32[2,16,16,1024]{3,2,0,1:T(8,128)} %copy.61), calls=%async_computation.1 | async-start | bytes 4194304 | tf_op jit(solution)/shard_map/all_to_all | solution.py:73
  126.4 2.6 %copy-start.9 = (f32[1024]{0:T(1024)S(1)}, f32[1024]{0:T(1024)}, u32[]{:S(2)}) copy-start(f32[1024]{0:T(1024)} %param.30) | copy-start | bytes 12292
  126.4 2.6 %copy-start.10 = (f32[1024]{0:T(1024)S(1)}, f32[1024]{0:T(1024)}, u32[]{:S(2)}) copy-start(f32[1024]{0:T(1024)} %param.27) | copy-start | bytes 12292
  126.4 2.6 %copy-start.14 = (f32[2]{0:T(128)S(1)}, f32[2]{0:T(128)}, u32[]{:S(2)}) copy-start(f32[2]{0:T(128)} %param.28) | copy-start | bytes 28
  129.0 1.3 copy-start.8
  129.0 4.7 %copy-start.5 = (f32[1,32,8,1024]{3,2,1,0:T(8,128)S(1)}, f32[1,32,8,1024]{3,2,1,0:T(8,128)}, u32[]{:S(2)}) copy-start(f32[1,32,8,1024]{3,2,1,0:T(8,128)} %param.21) | copy-start | bytes 3145732
  130.3 3.4 %copy-start.2 = (f32[1024,1024]{1,0:T(8,128)S(1)}, f32[1024,1024]{1,0:T(8,128)}, u32[]{:S(2)}) copy-start(f32[1024,1024]{1,0:T(8,128)} %param.22) | copy-start | bytes 12582916
  154.8 20.8 %copy-start.6 = (f32[1,32,8]{1,2,0:T(8,128)S(1)}, f32[1,32,8]{1,2,0:T(8,128)}, u32[]{:S(2)}) copy-start(f32[1,32,8]{1,2,0:T(8,128)} %param.31) | copy-start | bytes 3076
  173.7 2.2 %copy-start.3 = (f32[2,32,1024,8]{2,3,1,0:T(8,128)S(1)}, f32[2,32,1024,8]{2,3,1,0:T(8,128)}, u32[]{:S(2)}) copy-start(f32[2,32,1024,8]{2,3,1,0:T(8,128)} %fusion.41) | copy-start | bytes 6291460
  173.7 2.9 %copy-start.4 = (f32[2,32,8,1024]{3,1,2,0:T(8,128)S(1)}, f32[2,32,8,1024]{3,1,2,0:T(8,128)}, u32[]{:S(2)}) copy-start(f32[2,32,8,1024]{3,1,2,0:T(8,128)} %fusion) | copy-start | bytes 6291460
where the time goes:
time: 193 us; the launch traced here: 190 us
  waiting for transfers between devices  69.6 us (36%)
  matrix products  47.5 us (25%)
  local copies, waits for them, and re-layouts  39.7 us (21%)
  starting transfers between devices  22.8 us (12%)
  other arithmetic  6.9 us (4%)
  between operations  3.06 us (2%)
    all_to_all x1, waiting for transfers between devices, local(): lax.all_to_all(values, 'slab', split_axis=0, concat_axis=0, tiled=True)  41.6 us
    gather x1, local copies, waits for them, and re-layouts, local(): jnp.take(cells, cell_idx.reshape(-1), axis=1)  21.3 us
    all_to_all x1, waiting for transfers between devices, local(): lax.all_to_all(mixed, 'slab', split_axis=1, concat_axis=2, tiled=True)  18.9 us
    dot_general x1, matrix products, hamiltonian_apply(): jnp.einsum('ij,kqjza->kqiza', kinetic_bond, wave, precision=exact_prec)  10.2 us
    dot_general x1, matrix products, hamiltonian_apply(): jnp.einsum('kqrza,ba->kqrzb', potential[None] * grid_wave, angular_dvr, p...  9.43 us
    unnamed x33, local copies, waits for them, and re-layouts  9.38 us
    all_to_all x1, waiting for transfers between devices, local(): lax.all_to_all(flat_wave, 'slab', split_axis=2, concat_axis=1, tiled=True)  9.12 us
    dot_general x1, matrix products, local(): surface = jnp.einsum('pt,kpta->kpa', weights, stencil, precision=exact_prec)  8.41 us
  transfers between devices with their start and end apart: 4, of which 3 were waited for; matrix products, arithmetic and copies ran while one was open for 40% of the time, Pallas kernels for 0%

commit v1 on v0

--- a/solution.py
+++ b/solution.py
@@ -140,6 +140,112 @@
     return (wave_next, surface_flux)
 
 
+def split_dot(onehot, values):
+    high = lax.reduce_precision(values, exponent_bits=8, mantissa_bits=7)
+    both = jnp.concatenate([high, values - high], axis=-1).astype(jnp.bfloat16)
+    out = jnp.dot(onehot, both, preferred_element_type=jnp.float32)
+    width = values.shape[-1]
+    return out[:, :width] + out[:, width:]
+
+
+def local_blocks(
+    wave_now,
+    wave_prev,
+    potential,
+    angular_dvr,
+    kinetic_radial,
+    kinetic_bond,
+    kinetic_third,
+    inv_moment,
+    rot_level,
+    helicity,
+    coriolis,
+    ladder,
+    damping,
+    strip_bond,
+    strip_third,
+    strip_weight,
+    strip_length,
+    strip_owner,
+    strip_cell,
+):
+    blocks, _, bond_pts, thirds, angles = wave_now.shape
+    devices = lax.axis_size("slab")
+    cells = bond_pts * thirds
+    points = strip_bond.shape[1]
+    cuts = devices // blocks
+    width = angles // cuts
+    high_prec = lax.Precision.HIGH
+    wave = wave_now.reshape(blocks, cells, angles)
+
+    live = jnp.arange(points, dtype=jnp.int32)[None, :] < strip_length[:, None]
+    weights = jnp.where(live[:, :, None], strip_weight, 0.0)[0].T
+    base = (strip_bond * thirds + strip_third).astype(jnp.float32)
+    target = (strip_owner[:, :, 0] * P_DEV + strip_cell).astype(jnp.float32)
+    table = jnp.concatenate([base, target, weights, jnp.zeros((2, points), jnp.float32)], axis=0)
+    packed = wave.reshape(blocks, cells, cuts, width).transpose(0, 2, 1, 3)
+    packed = packed.reshape(devices, cells, width)
+    packed = jnp.concatenate(
+        [packed, jnp.broadcast_to(table[None], (devices,) + table.shape)], axis=1
+    )
+    got = lax.all_to_all(packed, "slab", split_axis=0, concat_axis=0, tiled=True)
+    field = got[:, :cells]
+    info = got[:, cells:]
+
+    mixed = jnp.einsum("ij,jca->ica", kinetic_radial, field, precision=high_prec)
+    cell_iota = jnp.arange(cells, dtype=jnp.float32)[None, None, :]
+    stencil = sum(
+        jnp.where(cell_iota == info[:, 0, :, None] + float(t * thirds), info[:, 2 + t, :, None], 0.0)
+        for t in range(4)
+    )
+    surface = jnp.einsum("qpc,qca->qpa", stencil, field, precision=high_prec)
+    product_iota = jnp.arange(devices * P_DEV, dtype=jnp.float32)[:, None]
+    landing = (product_iota == info[:, 1, :].reshape(-1)[None, :]).astype(jnp.bfloat16)
+    flux = split_dot(landing, surface.reshape(devices * points, width))
+    back = jnp.concatenate([mixed, flux.reshape(devices, P_DEV, width)], axis=1)
+    back = lax.all_to_all(back, "slab", split_axis=0, concat_axis=0, tiled=True)
+    back = back.reshape(blocks, cuts, cells + P_DEV, width)
+    radial_term = back[:, :, :cells].transpose(0, 2, 1, 3).reshape(blocks, cells, angles)
+    surface_flux = back[:, :, cells:].transpose(0, 2, 1, 3).reshape(blocks, P_DEV, angles)
+
+    kinetic = (
+        kinetic_bond[:, None, :, None] * jnp.eye(thirds, dtype=jnp.float32)[None, :, None, :]
+        + jnp.eye(bond_pts, dtype=jnp.float32)[:, None, :, None] * kinetic_third[None, :, None, :]
+    ).reshape(cells, cells)
+    kinetic_term = jnp.einsum("cd,kda->kca", kinetic, wave, precision=high_prec)
+    grid_wave = jnp.einsum("kcb,ba->kca", wave, angular_dvr, precision=high_prec)
+    potential_term = jnp.einsum(
+        "kca,ba->kcb",
+        potential.reshape(1, cells, angles) * grid_wave,
+        angular_dvr,
+        precision=high_prec,
+    )
+    moment = inv_moment[0]
+    rotation_term = moment * (rot_level[None, None, :] + helicity[:, None, None]) * wave
+    padding = jnp.zeros((1,) + wave.shape[1:], jnp.float32)
+    couple = coriolis[:, None, None]
+    above = jnp.concatenate([wave[1:] * couple, padding], axis=0)
+    below = jnp.concatenate([padding, wave[:-1] * couple], axis=0)
+    coriolis_term = moment * ladder[None, None, :] * (above + below)
+    damp = damping.reshape(1, cells, 1)
+    own = kinetic_term + potential_term + rotation_term + coriolis_term
+    wave_next = damp * (0.5 * (radial_term + own) - damp * wave_prev.reshape(wave.shape))
+    return wave_next.reshape(wave_now.shape), surface_flux
+
+
+def plan(*args):
+    blocks, local_rows, _, _, angles = args[0].shape
+    devices = lax.axis_size("slab")
+    cuts = devices // blocks
+    fits = (
+        local_rows == 1
+        and devices % blocks == 0
+        and angles % max(cuts, 1) == 0
+        and angles // max(cuts, 1) == args[13].shape[1]
+    )
+    return local_blocks(*args) if fits else local(*args)
+
+
 def solution(mesh):
     in_specs = (
         P("groups", "slab", None, None, None),
@@ -163,4 +269,4 @@
         P("slab", None),
     )
     out_specs = (P("groups", "slab", None, None, None), P("groups", "slab", None))
-    return jax.shard_map(local, mesh=mesh, in_specs=in_specs, out_specs=out_specs, check_vma=False)
+    return jax.shard_map(plan, mesh=mesh, in_specs=in_specs, out_specs=out_specs, check_vma=False)

time: 193 us -> 153 us (0.79); the launches traced: 190 us -> 153 us
  blocking collectives: 0 us -> 55.1 us
  waiting for transfers between devices: 69.6 us -> 38.8 us
  matrix products: 47.5 us -> 24.5 us
  local copies, waits for them, and re-layouts: 39.7 us -> 20.1 us
  starting transfers between devices: 22.8 us -> 6.59 us
  other arithmetic: 6.9 us -> 4.76 us
    all_to_all x0 -> x1, blocking collectives: none -> 55.1 us  [local_blocks(): lax.all_to_all(packed, 'slab', split_axis=0, concat_axis=0, tiled=True)]
    all_to_all x4 -> x1, waiting for transfers between devices: 69.6 us -> 38.8 us  [local_blocks(): back = lax.all_to_all(back, 'slab', split_axis=0, concat_axis=0, tiled=True)]
    dot_general x10 -> x6, matrix products: 47.5 us -> 24.5 us  [the longest x1 6.42 us: local_blocks(): kinetic_term = jnp.einsum('cd,kda->kca', kinetic, wave, precision=high_prec)]
    gather x1 -> x0, local copies, waits for them, and re-layouts: 21.3 us -> none  [local(): jnp.take(cells, cell_idx.reshape(-1), axis=1)]
    all_to_all x4 -> x1, starting transfers between devices: 22.8 us -> 6.59 us  [local_blocks(): back = lax.all_to_all(back, 'slab', split_axis=0, concat_axis=0, tiled=True)]
    select_n x2 -> x0, other arithmetic: 4.18 us -> none  [local(): jnp.take(cells, cell_idx.reshape(-1), axis=1)]
    all_to_all x3 -> x0, local copies, waits for them, and re-layouts: 4.12 us -> none  [the longest x1 1.88 us: local(): lax.all_to_all(mixed, 'slab', split_axis=1, concat_axis=2, tiled=True)]
    add x6 -> x1, local copies, waits for them, and re-layouts: 0.49 us -> 4.18 us  [local_blocks(): kinetic_bond[:, None, :, None]]
  transfers between devices with their start and end apart: 4 -> 1, of which waited for: 3 -> 1; matrix products, arithmetic and copies ran while one was open for 40% -> 11% of each run, Pallas kernels for 0% -> 0%
where the time goes in v1:
time: 153 us
  blocking collectives  55.1 us (36%)
  waiting for transfers between devices  38.8 us (25%)
  matrix products  24.5 us (16%)
  local copies, waits for them, and re-layouts  20.1 us (13%)
  starting transfers between devices  6.59 us (4%)
  other arithmetic  4.76 us (3%)
  between operations  2.87 us (2%)
    all_to_all x1, blocking collectives, local_blocks(): lax.all_to_all(packed, 'slab', split_axis=0, concat_axis=0, tiled=True)  55.1 us
    all_to_all x1, waiting for transfers between devices, local_blocks(): back = lax.all_to_all(back, 'slab', split_axis=0, concat_axis=0, tiled=True)  38.8 us
    all_to_all x1, starting transfers between devices, local_blocks(): back = lax.all_to_all(back, 'slab', split_axis=0, concat_axis=0, tiled=True)  6.59 us
    dot_general x1, matrix products, local_blocks(): kinetic_term = jnp.einsum('cd,kda->kca', kinetic, wave, precision=high_prec)  6.42 us
    unnamed x33, local copies, waits for them, and re-layouts  6.16 us
    dot_general x1, matrix products, local_blocks(): surface = jnp.einsum('qpc,qca->qpa', stencil, field, precision=high_prec)  5.97 us
    dot_general x1, matrix products, local_blocks(): jnp.einsum('kca,ba->kcb', potential.reshape(1, cells, angles) * grid_wave...  5.03 us
    add x1, local copies, waits for them, and re-layouts, local_blocks(): kinetic_bond[:, None, :, None]  4.18 us
  transfers between devices with their start and end apart: 1, of which 1 were waited for; matrix products, arithmetic and copies ran while one was open for 11% of the time, Pallas kernels for 0%

profile of v1, /device:TPU:13, one launch (start us, length us, event | category | flops | bytes accessed | tf_op | source)
XLA Modules:
  0.0 152.8 jit_solution(8128203767145399898)
XLA Ops:
  1.3 2.1 %copy.45 = f32[64,8,8,128]{3,2,1,0:T(8,128)S(1)} copy(f32[64,8,8,128]{3,1,2,0:T(8,128)} %bitcast.97) | data formatting | bytes 4194304
  3.4 0.4 copy.34
  4.3 55.1 %all_to_all.10 = f32[16,264,128]{2,1,0:T(8,128)S(1)} all-to-all(f32[16,264,128]{2,1,0:T(8,128)S(1)} %pad_maximum_fusion.1), channel_id=1, replica_groups=mesh['groups'=2,'slab'=16] {'slab'}, dimensions={0} | all-to-all | bytes 4325376 | tf_op jit(solution)/shard_map/all_to_all | solution.py:191
  59.5 6.0 %fusion.19 = f32[16,128,128]{2,1,0:T(8,128)S(1)} fusion(f32[16,128]{1,0:T(8,128)S(1)} %bitcast.107, f32[16,128]{1,0:T(8,128)S(1)} %get-tuple-element.19, f32[16,128]{1,0:T(8,128)S(1)} %bitcast.108, f32[16,128]{1,0:T(8,128)S(1)} %get-tuple-element.20, f32[16,128]{1,0:T(8,128)S(1)} %bitcast.109, f32[16,128]{1,0:T(8,128)S(1)} %get-tuple-element.18, ...), kind=kOutput, calls=%fused_computation.27 | convolution fusion | flops 408420352 | bytes 3211264 | tf_op jit(solution)/shard_map/qpc,qca->qpa/dot_general | solution.py:201
  65.5 0.2 reduce-precision_convert_fusion
  65.7 1.4 fusion
  67.1 0.3 copy.37
  67.4 0.2 slice.64
  67.6 2.0 %fusion.29 = f32[16,256,128]{2,0,1:T(8,128)S(1)} fusion(f32[16,256,128]{2,1,0:T(8,128)S(1)} %slice.64, f32[16,16]{1,0:T(8,128)S(1)} %copy-done), kind=kOutput, calls=%fused_computation.39 | convolution fusion | flops 50331648 | bytes 4195328 | tf_op jit(solution)/shard_map/ij,jca->ica/dot_general | solution.py:195
  69.6 0.2 pad_maximum_fusion
  69.8 2.3 %copy.38 = f32[16,320,128]{2,1,0:T(8,128)} copy(f32[16,320,128]{2,0,1:T(8,128)S(1)} %pad_maximum_fusion) | data formatting | bytes 5242880 | tf_op jit(solution)/shard_map/concatenate | solution.py:205
  72.2 6.6 %all-to-all-start.1 = ((f32[16,320,128]{2,1,0:T(8,128)}), f32[16,320,128]{2,1,0:T(8,128)}, u32[]{:S(2)}, u32[]{:S(2)}) async-start(f32[16,320,128]{2,1,0:T(8,128)} %copy.38), calls=%async_computation.1 | async-start | bytes 5242880 | tf_op jit(solution)/shard_map/all_to_all | solution.py:206
  80.3 2.7 %multiply_add_fusion = f32[32,8,32,8]{3,2,1,0:T(8,128)} fusion(f32[8,8]{1,0:T(8,128)S(1)} %copy-done.8, f32[32,32]{1,0:T(8,128)S(1)} %fusion.46, f32[8,8]{1,0:T(8,128)S(1)} %fusion.48, f32[32,32]{1,0:T(8,128)S(1)} %copy-done.4), kind=kLoop, calls=%fused_computation.6 | loop fusion | flops 196608 | bytes 270848 | tf_op jit(solution)/shard_map/add | solution.py:212
  83.0 4.2 %reshape.202 = f32[256,256,1]{1,0,2:T(8,128)S(1)} reshape(f32[32,8,32,8]{3,2,1,0:T(8,128)} %multiply_add_fusion) | data formatting | bytes 524288 | tf_op jit(solution)/shard_map/add | solution.py:212
  87.3 1.3 multiply_bitcast_fusion.1
  88.6 1.3 copy-done.2
  89.9 3.7 %fusion.3 = f32[2,256,1024]{2,1,0:T(8,128)S(1)} fusion(f32[1024,1024]{1,0:T(8,128)S(1)} %copy-done.2, f32[2,1,32,8,1024]{4,3,2,1,0:T(8,128)S(1)} %copy-done.1), kind=kOutput, calls=%fused_computation.4 | convolution fusion | flops 3221225472 | bytes 8388608 | tf_op jit(solution)/shard_map/kcb,ba->kca/dot_general | solution.py:216
  93.6 5.0 %fusion.1 = f32[2,256,1024]{2,1,0:T(8,128)} fusion(f32[1024,1024]{1,0:T(8,128)S(1)} %copy-done.2, f32[2,256,1024]{2,1,0:T(8,128)S(1)} %fusion.3, f32[256,1024]{1,0:T(8,128)S(1)} %bitcast.102), kind=kOutput, calls=%fused_computation.2 | convolution fusion | flops 3221749760 | bytes 9437184 | tf_op jit(solution)/shard_map/kca,ba->kcb/dot_general | solution.py:217
  98.7 38.8 %all-to-all-done.1 = f32[16,320,128]{2,1,0:T(8,128)} async-done(((f32[16,320,128]{2,1,0:T(8,128)}), f32[16,320,128]{2,1,0:T(8,128)}, u32[]{:S(2)}, u32[]{:S(2)}) %all-to-all-start.1) | async-done | bytes 2621472 | tf_op jit(solution)/shard_map/all_to_all | solution.py:206
  137.5 1.9 %copy_bitcast_fusion.1 = f32[2,64,1024]{2,1,0:T(8,128)} fusion(f32[2,8,320,128]{3,2,1,0:T(8,128)} %bitcast.16), kind=kLoop, calls=%fused_computation.58 | loop fusion | bytes 1048576 | tf_op jit(solution)/shard_map/reshape | solution.py:209
  139.4 1.7 %slice.73 = f32[2,8,256,128]{3,2,1,0:T(8,128)S(1)} slice(f32[2,8,320,128]{3,2,1,0:T(8,128)} %bitcast.16), slice={[0:2], [0:8], [0:256], [0:128]} | slice | bytes 4194304 | tf_op jit(solution)/shard_map/slice | solution.py:208
  141.2 2.5 %copy.52 = f32[2,8,256,128]{3,1,2,0:T(8,128)} copy(f32[2,8,256,128]{3,2,1,0:T(8,128)S(1)} %slice.73) | data formatting | bytes 4194304
  143.7 2.7 %reshape.196 = f32[2,256,1024]{2,1,0:T(8,128)} reshape(f32[2,256,8,128]{3,2,1,0:T(8,128)} %bitcast.99) | data formatting | bytes 4194304 | tf_op jit(solution)/shard_map/reshape | solution.py:208
  146.4 6.4 %fusion.10 = f32[2,1,32,8,1024]{4,3,2,1,0:T(8,128)} fusion(f32[2,1,32,8,1024]{4,3,2,1,0:T(8,128)} %param.20, f32[2,256,1024]{2,1,0:T(8,128)} %reshape.196, f32[2,256,1024]{2,1,0:T(8,128)} %fusion.1, f32[2,1,32,8,1024]{4,3,2,1,0:T(8,128)S(1)} %copy-done.1, f32[1,256,1024]{2,1,0:T(8,128)} %get-tuple-element.15, f32[1,256,1024]{2,1,0:T(8,128)S(1)} %get-tuple-element.14, ...), kind=kOutput, calls=%fused_computation.16 | convolution fusion | flops 811073536 | bytes 12858368 | tf_op jit(solution)/shard_map/cd,kda->kca/dot_general | solution.py:215
  (46 shorter events, 0.9 us)
Async XLA Ops:
  0.6 67.0 %copy-start = (f32[16,16]{1,0:T(8,128)S(1)}, f32[16,16]{1,0:T(8,128)}, u32[]{:S(2)}) copy-start(f32[16,16]{1,0:T(8,128)} %param.23) | copy-start | bytes 3076
  3.4 0.7 copy-start.9
  3.4 0.7 copy-start.10
  3.4 0.7 copy-start.11
  3.4 0.7 copy-start.12
  3.4 0.7 copy-start.13
  72.1 7.9 %copy-start.5 = (f32[1,32,8]{1,2,0:T(8,128)S(1)}, f32[1,32,8]{1,2,0:T(8,128)}, u32[]{:S(2)}) copy-start(f32[1,32,8]{1,2,0:T(8,128)} %param.31) | copy-start | bytes 3076
  72.1 8.1 %copy-start.4 = (f32[32,32]{1,0:T(8,128)S(1)}, f32[32,32]{1,0:T(8,128)}, u32[]{:S(2)}) copy-start(f32[32,32]{1,0:T(8,128)} %param.24) | copy-start | bytes 12292
  72.1 8.1 %copy-start.8 = (f32[8,8]{1,0:T(8,128)S(1)}, f32[8,8]{1,0:T(8,128)}, u32[]{:S(2)}) copy-start(f32[8,8]{1,0:T(8,128)} %param.25) | copy-start | bytes 772
  72.2 65.4 %all-to-all-start.1 = ((f32[16,320,128]{2,1,0:T(8,128)}), f32[16,320,128]{2,1,0:T(8,128)}, u32[]{:S(2)}, u32[]{:S(2)}) async-start(f32[16,320,128]{2,1,0:T(8,128)} %copy.38), calls=%async_computation.1 | async-start | bytes 5242880 | tf_op jit(solution)/shard_map/all_to_all | solution.py:206
  83.0 4.2 %copy-start.6 = (f32[1024]{0:T(1024)S(1)}, f32[1024]{0:T(1024)}, u32[]{:S(2)}) copy-start(f32[1024]{0:T(1024)} %param.30) | copy-start | bytes 12292
  83.0 4.2 %copy-start.7 = (f32[1024]{0:T(1024)S(1)}, f32[1024]{0:T(1024)}, u32[]{:S(2)}) copy-start(f32[1024]{0:T(1024)} %param.27) | copy-start | bytes 12292
  83.0 4.2 %copy-start.14 = (f32[2]{0:T(128)S(1)}, f32[2]{0:T(128)}, u32[]{:S(2)}) copy-start(f32[2]{0:T(128)} %param.28) | copy-start | bytes 28
  83.0 4.3 %copy-start.1 = (f32[2,1,32,8,1024]{4,3,2,1,0:T(8,128)S(1)}, f32[2,1,32,8,1024]{4,3,2,1,0:T(8,128)}, u32[]{:S(2)}) copy-start(f32[2,1,32,8,1024]{4,3,2,1,0:T(8,128)} %param.19) | copy-start | bytes 6291460
  87.3 2.6 %copy-start.2 = (f32[1024,1024]{1,0:T(8,128)S(1)}, f32[1024,1024]{1,0:T(8,128)}, u32[]{:S(2)}) copy-start(f32[1024,1024]{1,0:T(8,128)} %param.22) | copy-start | bytes 12582916
  89.9 3.7 %copy-start.3 = (f32[1,32,8,1024]{3,2,1,0:T(8,128)S(1)}, f32[1,32,8,1024]{3,2,1,0:T(8,128)}, u32[]{:S(2)}) copy-start(f32[1,32,8,1024]{3,2,1,0:T(8,128)} %param.21) | copy-start | bytes 3145732

commit v2 on v1

--- a/solution.py
+++ b/solution.py
@@ -1,6 +1,8 @@
 import jax
 import jax.numpy as jnp
 from jax import lax
+from jax.experimental import pallas as pl
+from jax.experimental.pallas import tpu as pltpu
 from jax.sharding import PartitionSpec as P
 
 SMAX = 128
@@ -146,6 +148,44 @@
     out = jnp.dot(onehot, both, preferred_element_type=jnp.float32)
     width = values.shape[-1]
     return out[:, :width] + out[:, width:]
+
+
+def finish_kernel(back_ref, own_ref, prev_ref, damp_ref, next_ref, flux_ref):
+    cells = own_ref.shape[1]
+    cuts = back_ref.shape[0]
+    width = back_ref.shape[2]
+    damp = damp_ref[...]
+    for cut in range(cuts):
+        lanes = slice(cut * width, (cut + 1) * width)
+        total = back_ref[cut, :cells, :] + own_ref[0, :, lanes]
+        next_ref[0, :, lanes] = damp * (0.5 * total - damp * prev_ref[0, :, lanes])
+        flux_ref[0, :, lanes] = back_ref[cut, cells:, :]
+
+
+def finish(back, own, prev, damp):
+    blocks, cells, angles = own.shape
+    devices, rows, width = back.shape
+    parts = 2
+    cuts = devices // blocks // parts
+    whole = pl.BlockSpec((1, cells, cuts * width), lambda k, h: (k, 0, h))
+    return pl.pallas_call(
+        finish_kernel,
+        grid=(blocks, parts),
+        in_specs=[
+            pl.BlockSpec((cuts, rows, width), lambda k, h: (k * parts + h, 0, 0)),
+            whole,
+            whole,
+            pl.BlockSpec((cells, 1), lambda k, h: (0, 0)),
+        ],
+        out_specs=[
+            whole,
+            pl.BlockSpec((1, rows - cells, cuts * width), lambda k, h: (k, 0, h)),
+        ],
+        out_shape=[
+            jax.ShapeDtypeStruct((blocks, cells, angles), jnp.float32),
+            jax.ShapeDtypeStruct((blocks, rows - cells, angles), jnp.float32),
+        ],
+    )(back, own, prev, damp)
 
 
 def local_blocks(
@@ -204,9 +244,6 @@
     flux = split_dot(landing, surface.reshape(devices * points, width))
     back = jnp.concatenate([mixed, flux.reshape(devices, P_DEV, width)], axis=1)
     back = lax.all_to_all(back, "slab", split_axis=0, concat_axis=0, tiled=True)
-    back = back.reshape(blocks, cuts, cells + P_DEV, width)
-    radial_term = back[:, :, :cells].transpose(0, 2, 1, 3).reshape(blocks, cells, angles)
-    surface_flux = back[:, :, cells:].transpose(0, 2, 1, 3).reshape(blocks, P_DEV, angles)
 
     kinetic = (
         kinetic_bond[:, None, :, None] * jnp.eye(thirds, dtype=jnp.float32)[None, :, None, :]
@@ -227,9 +264,10 @@
     above = jnp.concatenate([wave[1:] * couple, padding], axis=0)
     below = jnp.concatenate([padding, wave[:-1] * couple], axis=0)
     coriolis_term = moment * ladder[None, None, :] * (above + below)
-    damp = damping.reshape(1, cells, 1)
     own = kinetic_term + potential_term + rotation_term + coriolis_term
-    wave_next = damp * (0.5 * (radial_term + own) - damp * wave_prev.reshape(wave.shape))
+    wave_next, surface_flux = finish(
+        back, own, wave_prev.reshape(wave.shape), damping.reshape(cells, 1)
+    )
     return wave_next.reshape(wave_now.shape), surface_flux
 
 
@@ -242,6 +280,7 @@
         and devices % blocks == 0
         and angles % max(cuts, 1) == 0
         and angles // max(cuts, 1) == args[13].shape[1]
+        and cuts % 2 == 0
     )
     return local_blocks(*args) if fits else local(*args)
 

time: 153 us -> 143 us (0.935)
  local copies, waits for them, and re-layouts: 20.1 us -> 10.7 us
  Pallas kernels: 0 us -> 5.09 us
  matrix products: 24.5 us -> 19.8 us
  waiting for transfers between devices: 38.8 us -> 37 us
    pallas_call x0 -> x1, Pallas kernels: none -> 5.09 us  [finish(): pl.pallas_call(finish_kernel, grid=(blocks, parts), in_specs=[pl.BlockSpe...]
    reshape x3 -> x1, local copies, waits for them, and re-layouts: 4.92 us -> 0.75 us  [local_blocks(): damping.reshape(cells, 1)]
    dot_general x1, matrix products: 6.42 us -> 3.01 us  [local_blocks(): kinetic_term = jnp.einsum('cd,kda->kca', kinetic, wave, precision=high_prec)]
    concatenate x1 -> x0, local copies, waits for them, and re-layouts: 2.33 us -> none  [local_blocks(): back = jnp.concatenate([mixed, flux.reshape(devices, P_DEV, width)], axis=1)]
    all_to_all x1, waiting for transfers between devices: 38.8 us -> 37 us  [local_blocks(): back = lax.all_to_all(back, 'slab', split_axis=0, concat_axis=0, tiled=True)]
    unnamed x33 -> x32, local copies, waits for them, and re-layouts: 6.16 us -> 4.32 us
    slice x1 -> x0, local copies, waits for them, and re-layouts: 1.74 us -> none  [local_blocks(): back[:, :, :cells].transpose(0, 2, 1, 3).reshape(blocks, cells, angles)]
    concatenate x1, other arithmetic: 0.17 us -> 1.76 us  [local_blocks(): back = jnp.concatenate([mixed, flux.reshape(devices, P_DEV, width)], axis=1)]
  transfers between devices with their start and end apart: 1 -> 1, of which waited for: 1 -> 1; matrix products, arithmetic and copies ran while one was open for 11% -> 13% of each run, Pallas kernels for 0% -> 0%
where the time goes in v2:
time: 143 us; the launch traced here: 142 us
  blocking collectives  55.1 us (39%)
  waiting for transfers between devices  37 us (26%)
  matrix products  19.8 us (14%)
  local copies, waits for them, and re-layouts  10.7 us (7%)
  starting transfers between devices  6.6 us (5%)
  other arithmetic  5.25 us (4%)
  Pallas kernels  5.09 us (4%)
  between operations  2.85 us (2%)
    all_to_all x1, blocking collectives, local_blocks(): lax.all_to_all(packed, 'slab', split_axis=0, concat_axis=0, tiled=True)  55.1 us
    all_to_all x1, waiting for transfers between devices, local_blocks(): back = lax.all_to_all(back, 'slab', split_axis=0, concat_axis=0, tiled=True)  37 us
    all_to_all x1, starting transfers between devices, local_blocks(): back = lax.all_to_all(back, 'slab', split_axis=0, concat_axis=0, tiled=True)  6.6 us
    dot_general x1, matrix products, local_blocks(): surface = jnp.einsum('qpc,qca->qpa', stencil, field, precision=high_prec)  5.97 us
    pallas_call x1, Pallas kernels, finish(): pl.pallas_call(finish_kernel, grid=(blocks, parts), in_specs=[pl.BlockSpe...  5.09 us
    unnamed x32, local copies, waits for them, and re-layouts  4.32 us
    add x1, local copies, waits for them, and re-layouts, local_blocks(): kinetic_bond[:, None, :, None]  4.18 us
    dot_general x1, matrix products, local_blocks(): jnp.einsum('kcb,ba->kca', wave, angular_dvr, precision=high_prec)  3.73 us
  transfers between devices with their start and end apart: 1, of which 1 were waited for; matrix products, arithmetic and copies ran while one was open for 13% of the time, Pallas kernels for 0%

profile of v2, /device:TPU:13, one launch (start us, length us, event | category | flops | bytes accessed | tf_op | source)
XLA Modules:
  0.0 142.3 jit_solution(1058531826638343373)
XLA Ops:
  1.3 2.1 %copy.40 = f32[64,8,8,128]{3,2,1,0:T(8,128)S(1)} copy(f32[64,8,8,128]{3,1,2,0:T(8,128)} %bitcast.72) | data formatting | bytes 4194304
  3.4 0.4 copy.32
  3.9 0.2 copy-done.9
  4.1 0.1 pad.11.clone
  4.3 0.2 pad_maximum_fusion.1
  4.4 55.1 %all_to_all.10 = f32[16,264,128]{2,1,0:T(8,128)S(1)} all-to-all(f32[16,264,128]{2,1,0:T(8,128)S(1)} %pad_maximum_fusion.1), channel_id=1, replica_groups=mesh['groups'=2,'slab'=16] {'slab'}, dimensions={0} | all-to-all | bytes 4325376 | tf_op jit(solution)/shard_map/all_to_all | solution.py:231
  59.6 6.0 %fusion.14 = f32[16,128,128]{2,1,0:T(8,128)S(1)} fusion(f32[16,128]{1,0:T(8,128)S(1)} %bitcast.83, f32[16,128]{1,0:T(8,128)S(1)} %get-tuple-element.23, f32[16,128]{1,0:T(8,128)S(1)} %bitcast.84, f32[16,128]{1,0:T(8,128)S(1)} %get-tuple-element.24, f32[16,128]{1,0:T(8,128)S(1)} %bitcast.85, f32[16,128]{1,0:T(8,128)S(1)} %get-tuple-element.22, ...), kind=kOutput, calls=%fused_computation.21 | convolution fusion | flops 408420352 | bytes 3211264 | tf_op jit(solution)/shard_map/qpc,qca->qpa/dot_general | solution.py:241
  65.6 0.2 reduce-precision_convert_fusion
  65.7 1.4 fusion
  67.2 0.2 slice.56
  67.4 2.0 %fusion.6 = f32[256,128,16]{1,2,0:T(8,128)S(1)} fusion(f32[16,256,128]{2,1,0:T(8,128)S(1)} %slice.56, f32[16,16]{1,0:T(8,128)S(1)} %copy-done), kind=kOutput, calls=%fused_computation.10 | convolution fusion | flops 50331648 | bytes 4195328 | tf_op jit(solution)/shard_map/ij,jca->ica/dot_general | solution.py:235
  69.4 0.7 copy.44
  70.1 1.8 %pad_maximum_fusion = f32[16,320,128]{2,1,0:T(8,128)} fusion(f32[16,64,128]{2,1,0:T(8,128)S(1)} %bitcast.76, f32[16,256,128]{2,1,0:T(8,128)S(1)} %bitcast.74), kind=kLoop, calls=%fused_computation.8 | loop fusion | flops 655360 | bytes 5242880 | tf_op jit(solution)/shard_map/concatenate | solution.py:245
  71.9 6.6 %all-to-all-start.1 = ((f32[16,320,128]{2,1,0:T(8,128)}), f32[16,320,128]{2,1,0:T(8,128)}, u32[]{:S(2)}, u32[]{:S(2)}) async-start(f32[16,320,128]{2,1,0:T(8,128)} %pad_maximum_fusion), calls=%async_computation.1 | async-start | bytes 5242880 | tf_op jit(solution)/shard_map/all_to_all | solution.py:246
  79.8 2.7 %multiply_add_fusion = f32[32,8,32,8]{3,2,1,0:T(8,128)} fusion(f32[8,8]{1,0:T(8,128)S(1)} %copy-done.8, f32[32,32]{1,0:T(8,128)S(1)} %fusion.38, f32[8,8]{1,0:T(8,128)S(1)} %fusion.40, f32[32,32]{1,0:T(8,128)S(1)} %copy-done.4), kind=kLoop, calls=%fused_computation.6 | loop fusion | flops 196608 | bytes 270848 | tf_op jit(solution)/shard_map/add | solution.py:249
  82.5 4.2 %reshape.192 = f32[256,256,1]{1,0,2:T(8,128)S(1)} reshape(f32[32,8,32,8]{3,2,1,0:T(8,128)} %multiply_add_fusion) | data formatting | bytes 524288 | tf_op jit(solution)/shard_map/add | solution.py:249
  86.8 0.8 reshape.195.damp_ref
  87.6 0.3 multiply_bitcast_fusion.1
  87.9 1.9 %copy-done.2 = f32[1024,1024]{1,0:T(8,128)S(1)} copy-done((f32[1024,1024]{1,0:T(8,128)S(1)}, f32[1024,1024]{1,0:T(8,128)}, u32[]{:S(2)}) %copy-start.2) | copy-done | bytes 4194328
  89.8 3.7 %fusion.3 = f32[2,256,1024]{2,1,0:T(8,128)S(1)} fusion(f32[1024,1024]{1,0:T(8,128)S(1)} %copy-done.2, f32[2,1,32,8,1024]{4,3,2,1,0:T(8,128)S(1)} %copy-done.1), kind=kOutput, calls=%fused_computation.4 | convolution fusion | flops 3221225472 | bytes 8388608 | tf_op jit(solution)/shard_map/kcb,ba->kca/dot_general | solution.py:253
  93.5 3.7 %fusion.1 = f32[2,256,1024]{2,1,0:T(8,128)S(1)} fusion(f32[1024,1024]{1,0:T(8,128)S(1)} %copy-done.2, f32[2,256,1024]{2,1,0:T(8,128)S(1)} %fusion.3, f32[256,1024]{1,0:T(8,128)S(1)} %bitcast.78), kind=kOutput, calls=%fused_computation.2 | convolution fusion | flops 3221749760 | bytes 9437184 | tf_op jit(solution)/shard_map/kca,ba->kcb/dot_general | solution.py:254
  97.3 3.0 %fusion.9.own_ref = f32[2,256,1024]{2,1,0:T(8,128)} fusion(f32[2,256,1024]{2,1,0:T(8,128)S(1)} %fusion.1, f32[2,1,32,8,1024]{4,3,2,1,0:T(8,128)S(1)} %copy-done.1, f32[1,256,1024]{2,1,0:T(8,128)S(1)} %get-tuple-element.19, f32[1,256,1024]{2,1,0:T(8,128)S(1)} %get-tuple-element.18, f32[256,256,1]{1,0,2:T(8,128)S(1)} %reshape.192, ...), kind=kOutput, calls=%fused_computation.14 | convolution fusion | flops 808452096 | bytes 8663040 | tf_op jit(solution)/shard_map/cd,kda->kca/dot_general | solution.py:252
  100.3 37.0 %all-to-all-done.1.back_ref = f32[16,320,128]{2,1,0:T(8,128)} async-done(((f32[16,320,128]{2,1,0:T(8,128)}), f32[16,320,128]{2,1,0:T(8,128)}, u32[]{:S(2)}, u32[]{:S(2)}) %all-to-all-start.1) | async-done | bytes 2621472 | tf_op jit(solution)/shard_map/all_to_all | solution.py:246
  137.2 5.1 %shard_map.194 = (f32[2,256,1024]{2,1,0:T(8,128)}, f32[2,64,1024]{2,1,0:T(8,128)}) custom-call(f32[16,320,128]{2,1,0:T(8,128)} %all-to-all-done.1.back_ref, f32[2,256,1024]{2,1,0:T(8,128)} %fusion.9.own_ref, f32[2,256,1024]{2,1,0:T(8,128)} %bitcast.77, f32[256,1]{1,0:T(8,128)} %reshape.195.damp_ref), custom_call_target="tpu_custom_call" | custom-call | tf_op jit(solution)/shard_map/pallas_call | solution.py:171
  (42 shorter events, 0.4 us)
Async XLA Ops:
  0.6 66.8 %copy-start = (f32[16,16]{1,0:T(8,128)S(1)}, f32[16,16]{1,0:T(8,128)}, u32[]{:S(2)}) copy-start(f32[16,16]{1,0:T(8,128)} %param.23) | copy-start | bytes 3076
  3.4 0.7 copy-start.9
  3.4 0.8 copy-start.10
  3.4 0.7 copy-start.11
  3.4 0.7 copy-start.12
  3.4 0.7 copy-start.13
  71.9 7.9 %copy-start.4 = (f32[32,32]{1,0:T(8,128)S(1)}, f32[32,32]{1,0:T(8,128)}, u32[]{:S(2)}) copy-start(f32[32,32]{1,0:T(8,128)} %param.24) | copy-start | bytes 12292
  71.9 7.9 %copy-start.8 = (f32[8,8]{1,0:T(8,128)S(1)}, f32[8,8]{1,0:T(8,128)}, u32[]{:S(2)}) copy-start(f32[8,8]{1,0:T(8,128)} %param.25) | copy-start | bytes 772
  71.9 65.4 %all-to-all-start.1 = ((f32[16,320,128]{2,1,0:T(8,128)}), f32[16,320,128]{2,1,0:T(8,128)}, u32[]{:S(2)}, u32[]{:S(2)}) async-start(f32[16,320,128]{2,1,0:T(8,128)} %pad_maximum_fusion), calls=%async_computation.1 | async-start | bytes 5242880 | tf_op jit(solution)/shard_map/all_to_all | solution.py:246
  82.5 4.2 %copy-start.5 = (f32[1,32,8]{1,2,0:T(8,128)S(1)}, f32[1,32,8]{1,2,0:T(8,128)}, u32[]{:S(2)}) copy-start(f32[1,32,8]{1,2,0:T(8,128)} %param.31) | copy-start | bytes 3076
  82.5 5.1 %copy-start.6 = (f32[1024]{0:T(1024)S(1)}, f32[1024]{0:T(1024)}, u32[]{:S(2)}) copy-start(f32[1024]{0:T(1024)} %param.30) | copy-start | bytes 12292
  82.5 5.1 %copy-start.7 = (f32[1024]{0:T(1024)S(1)}, f32[1024]{0:T(1024)}, u32[]{:S(2)}) copy-start(f32[1024]{0:T(1024)} %param.27) | copy-start | bytes 12292
  82.5 5.1 %copy-start.14 = (f32[2]{0:T(128)S(1)}, f32[2]{0:T(128)}, u32[]{:S(2)}) copy-start(f32[2]{0:T(128)} %param.28) | copy-start | bytes 28
  82.5 5.1 %copy-start.1 = (f32[2,1,32,8,1024]{4,3,2,1,0:T(8,128)S(1)}, f32[2,1,32,8,1024]{4,3,2,1,0:T(8,128)}, u32[]{:S(2)}) copy-start(f32[2,1,32,8,1024]{4,3,2,1,0:T(8,128)} %param.19) | copy-start | bytes 6291460
  87.6 2.2 %copy-start.2 = (f32[1024,1024]{1,0:T(8,128)S(1)}, f32[1024,1024]{1,0:T(8,128)}, u32[]{:S(2)}) copy-start(f32[1024,1024]{1,0:T(8,128)} %param.22) | copy-start | bytes 12582916
  89.8 3.7 %copy-start.3 = (f32[1,32,8,1024]{3,2,1,0:T(8,128)S(1)}, f32[1,32,8,1024]{3,2,1,0:T(8,128)}, u32[]{:S(2)}) copy-start(f32[1,32,8,1024]{3,2,1,0:T(8,128)} %param.21) | copy-start | bytes 3145732

commit v3 on v2

--- a/solution.py
+++ b/solution.py
@@ -1,3 +1,5 @@
+import functools
+
 import jax
 import jax.numpy as jnp
 from jax import lax
@@ -186,6 +188,87 @@
             jax.ShapeDtypeStruct((blocks, rows - cells, angles), jnp.float32),
         ],
     )(back, own, prev, damp)
+
+
+def spread_kernel(devices, wave_ref, table_ref, field_ref, info_ref, send_sem, recv_sem, own_sem):
+    blocks, _, angles = wave_ref.shape
+    cuts = devices // blocks
+    width = angles // cuts
+    me = lax.axis_index("slab")
+    barrier = pltpu.get_barrier_semaphore()
+    for step in range(1, devices):
+        pl.semaphore_signal(
+            barrier,
+            inc=1,
+            device_id={"slab": lax.rem(me + step, devices)},
+            device_id_type=pl.DeviceIdType.MESH,
+        )
+
+    def block(peer):
+        lane = pl.multiple_of(lax.rem(peer, cuts) * width, width)
+        return wave_ref.at[peer // cuts, :, pl.ds(lane, width)]
+
+    own = [
+        pltpu.make_async_copy(block(me), field_ref.at[me], own_sem.at[0]),
+        pltpu.make_async_copy(table_ref, info_ref.at[me], own_sem.at[1]),
+    ]
+    for copy in own:
+        copy.start()
+    pl.semaphore_wait(barrier, devices - 1)
+
+    steps = sorted(range(1, devices), key=lambda step: abs(step - devices // 2))
+    copies = []
+    for step in steps:
+        peer = lax.rem(me + step, devices)
+        pairs = ((block(peer), field_ref.at[me]), (table_ref, info_ref.at[me]))
+        for part, (source, target) in enumerate(pairs):
+            copy = pltpu.make_async_remote_copy(
+                src_ref=source,
+                dst_ref=target,
+                send_sem=send_sem.at[part, step],
+                recv_sem=recv_sem.at[part, step],
+                device_id={"slab": peer},
+                device_id_type=pl.DeviceIdType.MESH,
+            )
+            copy.start()
+            copies.append(copy)
+    for copy in own:
+        copy.wait()
+    for step in steps:
+        sender = lax.rem(me + devices - step, devices)
+        pairs = ((block(me), field_ref.at[sender]), (table_ref, info_ref.at[sender]))
+        for part, (source, target) in enumerate(pairs):
+            pltpu.make_async_remote_copy(
+                src_ref=source,
+                dst_ref=target,
+                send_sem=send_sem.at[part, step],
+                recv_sem=recv_sem.at[part, step],
+                device_id={"slab": sender},
+                device_id_type=pl.DeviceIdType.MESH,
+            ).wait_recv()
+    for copy in copies:
+        copy.wait_send()
+
+
+def spread(wave, table):
+    blocks, cells, angles = wave.shape
+    devices = lax.axis_size("slab")
+    width = angles // (devices // blocks)
+    return pl.pallas_call(
+        functools.partial(spread_kernel, devices),
+        in_specs=[pl.BlockSpec(memory_space=pl.ANY)] * 2,
+        out_specs=[pl.BlockSpec(memory_space=pl.ANY)] * 2,
+        out_shape=[
+            jax.ShapeDtypeStruct((devices, cells, width), jnp.float32),
+            jax.ShapeDtypeStruct((devices,) + table.shape, jnp.float32),
+        ],
+        scratch_shapes=[
+            pltpu.SemaphoreType.DMA((2, devices)),
+            pltpu.SemaphoreType.DMA((2, devices)),
+            pltpu.SemaphoreType.DMA((2,)),
+        ],
+        compiler_params=pltpu.CompilerParams(collective_id=0, has_side_effects=True),
+    )(wave, table)
 
 
 def local_blocks(
@@ -223,14 +306,7 @@
     base = (strip_bond * thirds + strip_third).astype(jnp.float32)
     target = (strip_owner[:, :, 0] * P_DEV + strip_cell).astype(jnp.float32)
     table = jnp.concatenate([base, target, weights, jnp.zeros((2, points), jnp.float32)], axis=0)
-    packed = wave.reshape(blocks, cells, cuts, width).transpose(0, 2, 1, 3)
-    packed = packed.reshape(devices, cells, width)
-    packed = jnp.concatenate(
-        [packed, jnp.broadcast_to(table[None], (devices,) + table.shape)], axis=1
-    )
-    got = lax.all_to_all(packed, "slab", split_axis=0, concat_axis=0, tiled=True)
-    field = got[:, :cells]
-    info = got[:, cells:]
+    field, info = spread(wave, table)
 
     mixed = jnp.einsum("ij,jca->ica", kinetic_radial, field, precision=high_prec)
     cell_iota = jnp.arange(cells, dtype=jnp.float32)[None, None, :]

time: 143 us -> 137 us (0.958)
  blocking collectives: 55.1 us -> 0 us
  Pallas kernels: 5.09 us -> 57.4 us
  starting transfers between devices: 6.6 us -> 4.68 us
  other arithmetic: 5.25 us -> 7.09 us
  local copies, waits for them, and re-layouts: 10.7 us -> 8.96 us
    all_to_all x1 -> x0, blocking collectives: 55.1 us -> none  [local_blocks(): lax.all_to_all(packed, 'slab', split_axis=0, concat_axis=0, tiled=True)]
    pallas_call x0 -> x1, Pallas kernels: none -> 52.3 us  [spread(): pl.pallas_call(functools.partial(spread_kernel, devices), in_specs=[pl.Bl...]
    unnamed x32 -> x23, local copies, waits for them, and re-layouts: 4.32 us -> 2.16 us
    all_to_all x1, starting transfers between devices: 6.6 us -> 4.68 us  [local_blocks(): back = lax.all_to_all(back, 'slab', split_axis=0, concat_axis=0, tiled=True)]
  transfers between devices with their start and end apart: 1 -> 1, of which waited for: 1 -> 1; matrix products, arithmetic and copies ran while one was open for 13% -> 14% of each run, Pallas kernels for 0% -> 0%
where the time goes in v3:
time: 137 us
  Pallas kernels  57.4 us (42%)
  waiting for transfers between devices  36.9 us (27%)
  matrix products  18.7 us (14%)
  local copies, waits for them, and re-layouts  8.96 us (7%)
  other arithmetic  7.09 us (5%)
  starting transfers between devices  4.68 us (3%)
  between operations  2.79 us (2%)
    pallas_call x1, Pallas kernels, spread(): pl.pallas_call(functools.partial(spread_kernel, devices), in_specs=[pl.Bl...  52.3 us
    all_to_all x1, waiting for transfers between devices, local_blocks(): back = lax.all_to_all(back, 'slab', split_axis=0, concat_axis=0, tiled=True)  36.9 us
    pallas_call x1, Pallas kernels, finish(): pl.pallas_call(finish_kernel, grid=(blocks, parts), in_specs=[pl.BlockSpe...  5.09 us
    dot_general x1, matrix products, local_blocks(): surface = jnp.einsum('qpc,qca->qpa', stencil, field, precision=high_prec)  4.83 us
    all_to_all x1, starting transfers between devices, local_blocks(): back = lax.all_to_all(back, 'slab', split_axis=0, concat_axis=0, tiled=True)  4.68 us
    add x1, local copies, waits for them, and re-layouts, local_blocks(): kinetic_bond[:, None, :, None]  4.18 us
    dot_general x1, matrix products, local_blocks(): jnp.einsum('kcb,ba->kca', wave, angular_dvr, precision=high_prec)  3.73 us
    dot_general x1, matrix products, local_blocks(): jnp.einsum('kca,ba->kcb', potential.reshape(1, cells, angles) * grid_wave...  3.72 us
  transfers between devices with their start and end apart: 1, of which 1 were waited for; matrix products, arithmetic and copies ran while one was open for 14% of the time, Pallas kernels for 0%

profile of v3, /device:TPU:13, one launch (start us, length us, event | category | flops | bytes accessed | tf_op | source)
XLA Modules:
  0.0 136.5 jit_solution(6702096445770942193)
XLA Ops:
  1.3 0.7 select_bitcast_fusion
  2.0 0.1 pad.9.clone
  2.1 0.7 fusion.36
  2.8 0.7 maximum_maximum_fusion.table_ref
  3.5 52.3 %shard_map.194 = (f32[16,256,128]{2,1,0:T(8,128)}, f32[16,8,128]{2,1,0:T(8,128)}) custom-call(f32[2,256,1024]{2,1,0:T(8,128)} %bitcast.60, f32[8,128]{1,0:T(8,128)} %maximum_maximum_fusion.table_ref), custom_call_target="tpu_custom_call" | custom-call | tf_op jit(solution)/shard_map/pallas_call | solution.py:257
  55.8 1.1 fusion.41
  57.0 4.8 %fusion.11 = f32[16,128,128]{2,1,0:T(8,128)S(1)} fusion(f32[16,256,128]{2,1,0:T(8,128)} %get-tuple-element.6, f32[16,128]{1,0:T(8,128)S(1)} %bitcast.69, f32[16,128]{1,0:T(8,128)S(1)} %get-tuple-element.25, f32[16,128]{1,0:T(8,128)S(1)} %bitcast.70, f32[16,128]{1,0:T(8,128)S(1)} %get-tuple-element.26, f32[16,128]{1,0:T(8,128)S(1)} %bitcast.71, ...), kind=kOutput, calls=%fused_computation.16 | convolution fusion | flops 408420352 | bytes 3211264 | tf_op jit(solution)/shard_map/qpc,qca->qpa/dot_general | solution.py:317
  61.8 0.2 reduce-precision_convert_fusion
  62.0 1.4 fusion
  63.4 0.1 copy-done.3
  63.6 2.0 %fusion.8 = f32[256,128,16]{1,2,0:T(8,128)S(1)} fusion(f32[16,256,128]{2,1,0:T(8,128)S(1)} %copy-done.3, f32[16,16]{1,0:T(8,128)S(1)} %copy-done), kind=kOutput, calls=%fused_computation.13 | convolution fusion | flops 50331648 | bytes 4195328 | tf_op jit(solution)/shard_map/ij,jca->ica/dot_general | solution.py:311
  65.6 0.7 copy.33
  66.3 1.8 %pad_maximum_fusion = f32[16,320,128]{2,1,0:T(8,128)} fusion(f32[16,64,128]{2,1,0:T(8,128)S(1)} %bitcast.62, f32[16,256,128]{2,1,0:T(8,128)S(1)} %bitcast.61), kind=kLoop, calls=%fused_computation.8 | loop fusion | flops 655360 | bytes 5242880 | tf_op jit(solution)/shard_map/concatenate | solution.py:321
  68.0 4.7 %all-to-all-start = ((f32[16,320,128]{2,1,0:T(8,128)}), f32[16,320,128]{2,1,0:T(8,128)}, u32[]{:S(2)}, u32[]{:S(2)}) async-start(f32[16,320,128]{2,1,0:T(8,128)} %pad_maximum_fusion), calls=%async_computation | async-start | bytes 5242880 | tf_op jit(solution)/shard_map/all_to_all | solution.py:322
  74.1 2.7 %multiply_add_fusion = f32[32,8,32,8]{3,2,1,0:T(8,128)} fusion(f32[8,8]{1,0:T(8,128)S(1)} %copy-done.9, f32[32,32]{1,0:T(8,128)S(1)} %fusion.33, f32[8,8]{1,0:T(8,128)S(1)} %fusion.35, f32[32,32]{1,0:T(8,128)S(1)} %copy-done.5), kind=kLoop, calls=%fused_computation.6 | loop fusion | flops 196608 | bytes 270848 | tf_op jit(solution)/shard_map/add | solution.py:325
  76.7 4.2 %reshape.187 = f32[256,256,1]{1,0,2:T(8,128)S(1)} reshape(f32[32,8,32,8]{3,2,1,0:T(8,128)} %multiply_add_fusion) | data formatting | bytes 524288 | tf_op jit(solution)/shard_map/add | solution.py:325
  81.0 0.7 reshape.190.damp_ref
  81.9 0.3 multiply_bitcast_fusion.1
  82.1 1.9 %copy-done.2 = f32[1024,1024]{1,0:T(8,128)S(1)} copy-done((f32[1024,1024]{1,0:T(8,128)S(1)}, f32[1024,1024]{1,0:T(8,128)}, u32[]{:S(2)}) %copy-start.2) | copy-done | bytes 4194328
  84.0 3.7 %fusion.3 = f32[2,256,1024]{2,1,0:T(8,128)S(1)} fusion(f32[1024,1024]{1,0:T(8,128)S(1)} %copy-done.2, f32[2,1,32,8,1024]{4,3,2,1,0:T(8,128)S(1)} %copy-done.1), kind=kOutput, calls=%fused_computation.4 | convolution fusion | flops 3221225472 | bytes 8388608 | tf_op jit(solution)/shard_map/kcb,ba->kca/dot_general | solution.py:329
  87.8 3.7 %fusion.1 = f32[2,256,1024]{2,1,0:T(8,128)S(1)} fusion(f32[1024,1024]{1,0:T(8,128)S(1)} %copy-done.2, f32[2,256,1024]{2,1,0:T(8,128)S(1)} %fusion.3, f32[256,1024]{1,0:T(8,128)S(1)} %bitcast.64), kind=kOutput, calls=%fused_computation.2 | convolution fusion | flops 3221749760 | bytes 9437184 | tf_op jit(solution)/shard_map/kca,ba->kcb/dot_general | solution.py:330
  91.5 3.0 %fusion.7.own_ref = f32[2,256,1024]{2,1,0:T(8,128)} fusion(f32[2,256,1024]{2,1,0:T(8,128)S(1)} %fusion.1, f32[1,256,1024]{2,1,0:T(8,128)S(1)} %get-tuple-element.15, f32[1,256,1024]{2,1,0:T(8,128)S(1)} %get-tuple-element.14, f32[256,256,1]{1,0,2:T(8,128)S(1)} %reshape.187, f32[1024]{0:T(1024)S(1)} %broadcast_multiply_fusion, ...), kind=kOutput, calls=%fused_computation.11 | convolution fusion | flops 808452096 | bytes 8663040 | tf_op jit(solution)/shard_map/cd,kda->kca/dot_general | solution.py:328
  94.5 36.9 %all-to-all-done.back_ref = f32[16,320,128]{2,1,0:T(8,128)} async-done(((f32[16,320,128]{2,1,0:T(8,128)}), f32[16,320,128]{2,1,0:T(8,128)}, u32[]{:S(2)}, u32[]{:S(2)}) %all-to-all-start) | async-done | bytes 2621472 | tf_op jit(solution)/shard_map/all_to_all | solution.py:322
  131.4 5.1 %shard_map.195 = (f32[2,256,1024]{2,1,0:T(8,128)}, f32[2,64,1024]{2,1,0:T(8,128)}) custom-call(f32[16,320,128]{2,1,0:T(8,128)} %all-to-all-done.back_ref, f32[2,256,1024]{2,1,0:T(8,128)} %fusion.7.own_ref, f32[2,256,1024]{2,1,0:T(8,128)} %bitcast.63, f32[256,1]{1,0:T(8,128)} %reshape.190.damp_ref), custom_call_target="tpu_custom_call" | custom-call | tf_op jit(solution)/shard_map/pallas_call | solution.py:173
  (29 shorter events, 0.3 us)
Async XLA Ops:
  0.6 62.8 %copy-start = (f32[16,16]{1,0:T(8,128)S(1)}, f32[16,16]{1,0:T(8,128)}, u32[]{:S(2)}) copy-start(f32[16,16]{1,0:T(8,128)} %param.23) | copy-start | bytes 3076
  62.0 1.6 %copy-start.3 = (f32[16,256,128]{2,1,0:T(8,128)S(1)}, f32[16,256,128]{2,1,0:T(8,128)}, u32[]{:S(2)}) copy-start(f32[16,256,128]{2,1,0:T(8,128)} %get-tuple-element.6) | copy-start | bytes 6291460
  68.0 6.0 %copy-start.5 = (f32[32,32]{1,0:T(8,128)S(1)}, f32[32,32]{1,0:T(8,128)}, u32[]{:S(2)}) copy-start(f32[32,32]{1,0:T(8,128)} %param.24) | copy-start | bytes 12292
  68.0 6.0 %copy-start.9 = (f32[8,8]{1,0:T(8,128)S(1)}, f32[8,8]{1,0:T(8,128)}, u32[]{:S(2)}) copy-start(f32[8,8]{1,0:T(8,128)} %param.25) | copy-start | bytes 772
  68.0 63.4 %all-to-all-start = ((f32[16,320,128]{2,1,0:T(8,128)}), f32[16,320,128]{2,1,0:T(8,128)}, u32[]{:S(2)}, u32[]{:S(2)}) async-start(f32[16,320,128]{2,1,0:T(8,128)} %pad_maximum_fusion), calls=%async_computation | async-start | bytes 5242880 | tf_op jit(solution)/shard_map/all_to_all | solution.py:322
  76.7 4.2 %copy-start.6 = (f32[1,32,8]{1,2,0:T(8,128)S(1)}, f32[1,32,8]{1,2,0:T(8,128)}, u32[]{:S(2)}) copy-start(f32[1,32,8]{1,2,0:T(8,128)} %param.31) | copy-start | bytes 3076
  76.7 5.0 %copy-start.7 = (f32[1024]{0:T(1024)S(1)}, f32[1024]{0:T(1024)}, u32[]{:S(2)}) copy-start(f32[1024]{0:T(1024)} %param.30) | copy-start | bytes 12292
  76.7 5.0 %copy-start.8 = (f32[1024]{0:T(1024)S(1)}, f32[1024]{0:T(1024)}, u32[]{:S(2)}) copy-start(f32[1024]{0:T(1024)} %param.27) | copy-start | bytes 12292
  76.7 5.0 %copy-start.10 = (f32[2]{0:T(128)S(1)}, f32[2]{0:T(128)}, u32[]{:S(2)}) copy-start(f32[2]{0:T(128)} %param.28) | copy-start | bytes 28
  76.7 5.1 %copy-start.1 = (f32[2,1,32,8,1024]{4,3,2,1,0:T(8,128)S(1)}, f32[2,1,32,8,1024]{4,3,2,1,0:T(8,128)}, u32[]{:S(2)}) copy-start(f32[2,1,32,8,1024]{4,3,2,1,0:T(8,128)} %param.19) | copy-start | bytes 6291460
  81.9 2.2 %copy-start.2 = (f32[1024,1024]{1,0:T(8,128)S(1)}, f32[1024,1024]{1,0:T(8,128)}, u32[]{:S(2)}) copy-start(f32[1024,1024]{1,0:T(8,128)} %param.22) | copy-start | bytes 12582916
  84.0 3.7 %copy-start.4 = (f32[1,32,8,1024]{3,2,1,0:T(8,128)S(1)}, f32[1,32,8,1024]{3,2,1,0:T(8,128)}, u32[]{:S(2)}) copy-start(f32[1,32,8,1024]{3,2,1,0:T(8,128)} %param.21) | copy-start | bytes 3145732

commit v4 on v3

--- a/solution.py
+++ b/solution.py
@@ -152,21 +152,22 @@
     return out[:, :width] + out[:, width:]
 
 
-def finish_kernel(back_ref, own_ref, prev_ref, damp_ref, next_ref, flux_ref):
+def finish_kernel(back_ref, part_ref, own_ref, prev_ref, damp_ref, next_ref, flux_ref):
     cells = own_ref.shape[1]
     cuts = back_ref.shape[0]
     width = back_ref.shape[2]
     damp = damp_ref[...]
     for cut in range(cuts):
         lanes = slice(cut * width, (cut + 1) * width)
-        total = back_ref[cut, :cells, :] + own_ref[0, :, lanes]
+        total = back_ref[cut] + own_ref[0, :, lanes]
         next_ref[0, :, lanes] = damp * (0.5 * total - damp * prev_ref[0, :, lanes])
-        flux_ref[0, :, lanes] = back_ref[cut, cells:, :]
-
-
-def finish(back, own, prev, damp):
+        flux_ref[0, :, lanes] = part_ref[cut]
+
+
+def finish(back, flux, own, prev, damp):
     blocks, cells, angles = own.shape
-    devices, rows, width = back.shape
+    devices, _, width = back.shape
+    rows = flux.shape[1]
     parts = 2
     cuts = devices // blocks // parts
     whole = pl.BlockSpec((1, cells, cuts * width), lambda k, h: (k, 0, h))
@@ -174,6 +175,7 @@
         finish_kernel,
         grid=(blocks, parts),
         in_specs=[
+            pl.BlockSpec((cuts, cells, width), lambda k, h: (k * parts + h, 0, 0)),
             pl.BlockSpec((cuts, rows, width), lambda k, h: (k * parts + h, 0, 0)),
             whole,
             whole,
@@ -181,13 +183,13 @@
         ],
         out_specs=[
             whole,
-            pl.BlockSpec((1, rows - cells, cuts * width), lambda k, h: (k, 0, h)),
+            pl.BlockSpec((1, rows, cuts * width), lambda k, h: (k, 0, h)),
         ],
         out_shape=[
             jax.ShapeDtypeStruct((blocks, cells, angles), jnp.float32),
-            jax.ShapeDtypeStruct((blocks, rows - cells, angles), jnp.float32),
-        ],
-    )(back, own, prev, damp)
+            jax.ShapeDtypeStruct((blocks, rows, angles), jnp.float32),
+        ],
+    )(back, flux, own, prev, damp)
 
 
 def spread_kernel(devices, wave_ref, table_ref, field_ref, info_ref, send_sem, recv_sem, own_sem):
@@ -271,6 +273,77 @@
     )(wave, table)
 
 
+def return_kernel(devices, flux_ref, out_ref, send_sem, recv_sem, own_sem):
+    me = lax.axis_index("slab")
+    barrier = pltpu.get_barrier_semaphore()
+    for step in range(1, devices):
+        pl.semaphore_signal(
+            barrier,
+            inc=1,
+            device_id={"slab": lax.rem(me + step, devices)},
+            device_id_type=pl.DeviceIdType.MESH,
+        )
+
+    def block(peer):
+        return flux_ref.at[peer]
+
+    own = [
+        pltpu.make_async_copy(block(me), out_ref.at[me], own_sem.at[0]),
+    ]
+    for copy in own:
+        copy.start()
+    pl.semaphore_wait(barrier, devices - 1)
+
+    steps = sorted(range(1, devices), key=lambda step: abs(step - devices // 2))
+    copies = []
+    for step in steps:
+        peer = lax.rem(me + step, devices)
+        pairs = ((block(peer), out_ref.at[me]),)
+        for part, (source, target) in enumerate(pairs):
+            copy = pltpu.make_async_remote_copy(
+                src_ref=source,
+                dst_ref=target,
+                send_sem=send_sem.at[part, step],
+                recv_sem=recv_sem.at[part, step],
+                device_id={"slab": peer},
+                device_id_type=pl.DeviceIdType.MESH,
+            )
+            copy.start()
+            copies.append(copy)
+    for copy in own:
+        copy.wait()
+    for step in steps:
+        sender = lax.rem(me + devices - step, devices)
+        pairs = ((block(me), out_ref.at[sender]),)
+        for part, (source, target) in enumerate(pairs):
+            pltpu.make_async_remote_copy(
+                src_ref=source,
+                dst_ref=target,
+                send_sem=send_sem.at[part, step],
+                recv_sem=recv_sem.at[part, step],
+                device_id={"slab": sender},
+                device_id_type=pl.DeviceIdType.MESH,
+            ).wait_recv()
+    for copy in copies:
+        copy.wait_send()
+
+
+def send_back(flux):
+    devices = flux.shape[0]
+    return pl.pallas_call(
+        functools.partial(return_kernel, devices),
+        in_specs=[pl.BlockSpec(memory_space=pl.ANY)],
+        out_specs=pl.BlockSpec(memory_space=pl.ANY),
+        out_shape=jax.ShapeDtypeStruct(flux.shape, jnp.float32),
+        scratch_shapes=[
+            pltpu.SemaphoreType.DMA((1, devices)),
+            pltpu.SemaphoreType.DMA((1, devices)),
+            pltpu.SemaphoreType.DMA((1,)),
+        ],
+        compiler_params=pltpu.CompilerParams(collective_id=1, has_side_effects=True),
+    )(flux)
+
+
 def local_blocks(
     wave_now,
     wave_prev,
@@ -318,8 +391,8 @@
     product_iota = jnp.arange(devices * P_DEV, dtype=jnp.float32)[:, None]
     landing = (product_iota == info[:, 1, :].reshape(-1)[None, :]).astype(jnp.bfloat16)
     flux = split_dot(landing, surface.reshape(devices * points, width))
-    back = jnp.concatenate([mixed, flux.reshape(devices, P_DEV, width)], axis=1)
-    back = lax.all_to_all(back, "slab", split_axis=0, concat_axis=0, tiled=True)
+    back = lax.all_to_all(mixed, "slab", split_axis=0, concat_axis=0, tiled=True)
+    flux = send_back(flux.reshape(devices, P_DEV, width))
 
     kinetic = (
         kinetic_bond[:, None, :, None] * jnp.eye(thirds, dtype=jnp.float32)[None, :, None, :]
@@ -342,7 +415,7 @@
     coriolis_term = moment * ladder[None, None, :] * (above + below)
     own = kinetic_term + potential_term + rotation_term + coriolis_term
     wave_next, surface_flux = finish(
-        back, own, wave_prev.reshape(wave.shape), damping.reshape(cells, 1)
+        back, flux, own, wave_prev.reshape(wave.shape), damping.reshape(cells, 1)
     )
     return wave_next.reshape(wave_now.shape), surface_flux
 

time: 137 us -> 154 us (1.12)
  Pallas kernels: 57.4 us -> 108 us
  waiting for transfers between devices: 36.9 us -> 0.01 us
  matrix products: 18.7 us -> 21.3 us
    pallas_call x0 -> x1, Pallas kernels: none -> 50.6 us  [send_back(): pl.pallas_call(functools.partial(return_kernel, devices), in_specs=[pl.Bl...]
    all_to_all x1, waiting for transfers between devices: 36.9 us -> 0.01 us  [local_blocks(): lax.all_to_all(mixed, 'slab', split_axis=0, concat_axis=0, tiled=True)]
    concatenate x1 -> x0, other arithmetic: 1.76 us -> none  [local_blocks(): back = jnp.concatenate([mixed, flux.reshape(devices, P_DEV, width)], axis=1)]
  transfers between devices with their start and end apart: 1 -> 1, of which waited for: 1 -> 0; matrix products, arithmetic and copies ran while one was open for 14% -> 18% of each run, Pallas kernels for 0% -> 33%
where the time goes in v4:
time: 154 us; the launch traced here: 152 us
  Pallas kernels  108 us (70%)
  matrix products  21.3 us (14%)
  local copies, waits for them, and re-layouts  9.21 us (6%)
  other arithmetic  6.12 us (4%)
  starting transfers between devices  4.66 us (3%)
  between operations  2.8 us (2%)
    pallas_call x1, Pallas kernels, spread(): pl.pallas_call(functools.partial(spread_kernel, devices), in_specs=[pl.Bl...  52.3 us
    pallas_call x1, Pallas kernels, send_back(): pl.pallas_call(functools.partial(return_kernel, devices), in_specs=[pl.Bl...  50.6 us
    dot_general x1, matrix products, local_blocks(): surface = jnp.einsum('qpc,qca->qpa', stencil, field, precision=high_prec)  5.98 us
    pallas_call x1, Pallas kernels, finish(): pl.pallas_call(finish_kernel, grid=(blocks, parts), in_specs=[pl.BlockSpe...  5.18 us
    all_to_all x1, starting transfers between devices, local_blocks(): lax.all_to_all(mixed, 'slab', split_axis=0, concat_axis=0, tiled=True)  4.66 us
    add x1, local copies, waits for them, and re-layouts, local_blocks(): kinetic_bond[:, None, :, None]  4.36 us
    dot_general x1, matrix products, local_blocks(): jnp.einsum('kcb,ba->kca', wave, angular_dvr, precision=high_prec)  3.72 us
    dot_general x1, matrix products, local_blocks(): jnp.einsum('kca,ba->kcb', potential.reshape(1, cells, angles) * grid_wave...  3.72 us
  transfers between devices with their start and end apart: 1, of which 0 were waited for; matrix products, arithmetic and copies ran while one was open for 18% of the time, Pallas kernels for 33%

profile of v4, /device:TPU:13, one launch (start us, length us, event | category | flops | bytes accessed | tf_op | source)
XLA Modules:
  0.0 152.2 jit_solution(5469467610442193410)
XLA Ops:
  1.3 0.7 select_bitcast_fusion
  2.0 0.1 pad.7.clone
  2.1 0.7 fusion.36
  2.8 0.7 maximum_maximum_fusion.table_ref
  3.5 52.3 %shard_map.194 = (f32[16,256,128]{2,1,0:T(8,128)}, f32[16,8,128]{2,1,0:T(8,128)}) custom-call(f32[2,256,1024]{2,1,0:T(8,128)} %bitcast.60, f32[8,128]{1,0:T(8,128)} %maximum_maximum_fusion.table_ref), custom_call_target="tpu_custom_call" | custom-call | tf_op jit(solution)/shard_map/pallas_call | solution.py:259
  55.8 3.5 %fusion.8 = f32[256,128,16]{1,2,0:T(8,128)S(1)} fusion(f32[16,256,128]{2,1,0:T(8,128)} %get-tuple-element.6, f32[16,16]{1,0:T(8,128)S(1)} %copy-done), kind=kOutput, calls=%fused_computation.12 | convolution fusion | flops 50331648 | bytes 4195328 | tf_op jit(solution)/shard_map/ij,jca->ica/dot_general | solution.py:384
  59.3 2.0 %copy.33 = f32[256,128,16]{1,0,2:T(8,128)} copy(f32[256,128,16]{1,2,0:T(8,128)S(1)} %fusion.8) | data formatting | bytes 4194304 | tf_op jit(solution)/shard_map/ij,jca->ica/dot_general | solution.py:384
  61.3 4.7 %all-to-all-start = ((f32[16,256,128]{2,1,0:T(8,128)}), f32[16,256,128]{2,1,0:T(8,128)}, u32[]{:S(2)}, u32[]{:S(2)}) async-start(f32[16,256,128]{2,1,0:T(8,128)} %bitcast.55), calls=%async_computation | async-start | bytes 4194304 | tf_op jit(solution)/shard_map/all_to_all | solution.py:394
  66.0 6.0 %fusion.11 = f32[16,128,128]{2,1,0:T(8,128)S(1)} fusion(f32[16,256,128]{2,1,0:T(8,128)S(1)} %copy-done.3, f32[16,128]{1,0:T(8,128)S(1)} %bitcast.68, f32[16,128]{1,0:T(8,128)S(1)} %get-tuple-element.25, f32[16,128]{1,0:T(8,128)S(1)} %bitcast.69, f32[16,128]{1,0:T(8,128)S(1)} %get-tuple-element.26, f32[16,128]{1,0:T(8,128)S(1)} %bitcast.70, ...), kind=kOutput, calls=%fused_computation.15 | convolution fusion | flops 408420352 | bytes 3211264 | tf_op jit(solution)/shard_map/qpc,qca->qpa/dot_general | solution.py:390
  72.0 0.2 reduce-precision_convert_fusion
  72.2 1.4 fusion
  73.6 0.8 slice_add_fusion
  74.4 50.6 %shard_map.195.part_ref = f32[16,64,128]{2,1,0:T(8,128)} custom-call(f32[16,64,128]{2,1,0:T(8,128)} %bitcast.61), custom_call_target="tpu_custom_call" | custom-call | tf_op jit(solution)/shard_map/pallas_call | solution.py:333
  126.4 2.7 %multiply_add_fusion = f32[32,8,32,8]{3,2,1,0:T(8,128)} fusion(f32[8,8]{1,0:T(8,128)S(1)} %copy-done.10, f32[32,32]{1,0:T(8,128)S(1)} %fusion.33, f32[8,8]{1,0:T(8,128)S(1)} %fusion.35, f32[32,32]{1,0:T(8,128)S(1)} %copy-done.6), kind=kLoop, calls=%fused_computation.6 | loop fusion | flops 196608 | bytes 270848 | tf_op jit(solution)/shard_map/add | solution.py:398
  129.1 4.4 %reshape.187 = f32[256,256,1]{1,0,2:T(8,128)S(1)} reshape(f32[32,8,32,8]{3,2,1,0:T(8,128)} %multiply_add_fusion) | data formatting | bytes 524288 | tf_op jit(solution)/shard_map/add | solution.py:398
  133.4 0.1 copy.27
  133.5 0.7 reshape.190.damp_ref
  134.3 0.1 add_multiply_fusion
  134.4 0.3 multiply_bitcast_fusion.1
  134.7 1.9 %copy-done.2 = f32[1024,1024]{1,0:T(8,128)S(1)} copy-done((f32[1024,1024]{1,0:T(8,128)S(1)}, f32[1024,1024]{1,0:T(8,128)}, u32[]{:S(2)}) %copy-start.2) | copy-done | bytes 4194328
  136.6 3.7 %fusion.3 = f32[2,256,1024]{2,1,0:T(8,128)S(1)} fusion(f32[1024,1024]{1,0:T(8,128)S(1)} %copy-done.2, f32[2,1,32,8,1024]{4,3,2,1,0:T(8,128)S(1)} %copy-done.1), kind=kOutput, calls=%fused_computation.4 | convolution fusion | flops 3221225472 | bytes 8388608 | tf_op jit(solution)/shard_map/kcb,ba->kca/dot_general | solution.py:402
  140.3 3.7 %fusion.1 = f32[2,256,1024]{2,1,0:T(8,128)S(1)} fusion(f32[1024,1024]{1,0:T(8,128)S(1)} %copy-done.2, f32[2,256,1024]{2,1,0:T(8,128)S(1)} %fusion.3, f32[256,1024]{1,0:T(8,128)S(1)} %bitcast.63), kind=kOutput, calls=%fused_computation.2 | convolution fusion | flops 3221749760 | bytes 9437184 | tf_op jit(solution)/shard_map/kca,ba->kcb/dot_general | solution.py:403
  144.0 3.0 %fusion.7.own_ref = f32[2,256,1024]{2,1,0:T(8,128)} fusion(f32[2,256,1024]{2,1,0:T(8,128)S(1)} %fusion.1, f32[1,256,1024]{2,1,0:T(8,128)S(1)} %get-tuple-element.15, f32[1,256,1024]{2,1,0:T(8,128)S(1)} %get-tuple-element.14, f32[256,256,1]{1,0,2:T(8,128)S(1)} %reshape.187, f32[1024]{0:T(1024)S(1)} %broadcast_multiply_fusion, ...), kind=kOutput, calls=%fused_computation.10 | convolution fusion | flops 808452096 | bytes 8663040 | tf_op jit(solution)/shard_map/cd,kda->kca/dot_general | solution.py:401
  147.1 5.2 %shard_map.196 = (f32[2,256,1024]{2,1,0:T(8,128)}, f32[2,64,1024]{2,1,0:T(8,128)}) custom-call(f32[16,256,128]{2,1,0:T(8,128)} %all-to-all-done.back_ref, f32[16,64,128]{2,1,0:T(8,128)} %shard_map.195.part_ref, f32[2,256,1024]{2,1,0:T(8,128)} %fusion.7.own_ref, f32[2,256,1024]{2,1,0:T(8,128)} %bitcast.62, f32[256,1]{1,0:T(8,128)} %reshape.190.damp_ref), custom_call_target="tpu_custom_call" | custom-call | tf_op jit(solution)/shard_map/pallas_call | solution.py:174
  (31 shorter events, 0.1 us)
Async XLA Ops:
  0.6 55.2 %copy-start = (f32[16,16]{1,0:T(8,128)S(1)}, f32[16,16]{1,0:T(8,128)}, u32[]{:S(2)}) copy-start(f32[16,16]{1,0:T(8,128)} %param.23) | copy-start | bytes 3076
  61.3 4.7 %copy-start.5 = (f32[16,8,128]{2,1,0:T(8,128)S(1)}, f32[16,8,128]{2,1,0:T(8,128)}, u32[]{:S(2)}) copy-start(f32[16,8,128]{2,1,0:T(8,128)} %get-tuple-element.7) | copy-start | bytes 196612
  61.3 4.7 %copy-start.3 = (f32[16,256,128]{2,1,0:T(8,128)S(1)}, f32[16,256,128]{2,1,0:T(8,128)}, u32[]{:S(2)}) copy-start(f32[16,256,128]{2,1,0:T(8,128)} %get-tuple-element.6) | copy-start | bytes 6291460
  61.3 85.8 %all-to-all-start = ((f32[16,256,128]{2,1,0:T(8,128)}), f32[16,256,128]{2,1,0:T(8,128)}, u32[]{:S(2)}, u32[]{:S(2)}) async-start(f32[16,256,128]{2,1,0:T(8,128)} %bitcast.55), calls=%async_computation | async-start | bytes 4194304 | tf_op jit(solution)/shard_map/all_to_all | solution.py:394
  73.6 52.8 %copy-start.6 = (f32[32,32]{1,0:T(8,128)S(1)}, f32[32,32]{1,0:T(8,128)}, u32[]{:S(2)}) copy-start(f32[32,32]{1,0:T(8,128)} %param.24) | copy-start | bytes 12292
  73.6 52.8 %copy-start.10 = (f32[8,8]{1,0:T(8,128)S(1)}, f32[8,8]{1,0:T(8,128)}, u32[]{:S(2)}) copy-start(f32[8,8]{1,0:T(8,128)} %param.25) | copy-start | bytes 772
  129.0 4.4 %copy-start.7 = (f32[1,32,8]{1,2,0:T(8,128)S(1)}, f32[1,32,8]{1,2,0:T(8,128)}, u32[]{:S(2)}) copy-start(f32[1,32,8]{1,2,0:T(8,128)} %param.31) | copy-start | bytes 3076
  129.1 5.2 %copy-start.8 = (f32[1024]{0:T(1024)S(1)}, f32[1024]{0:T(1024)}, u32[]{:S(2)}) copy-start(f32[1024]{0:T(1024)} %param.30) | copy-start | bytes 12292
  129.1 5.2 %copy-start.9 = (f32[1024]{0:T(1024)S(1)}, f32[1024]{0:T(1024)}, u32[]{:S(2)}) copy-start(f32[1024]{0:T(1024)} %param.27) | copy-start | bytes 12292
  129.1 5.2 %copy-start.11 = (f32[2]{0:T(128)S(1)}, f32[2]{0:T(128)}, u32[]{:S(2)}) copy-start(f32[2]{0:T(128)} %param.28) | copy-start | bytes 28
  129.1 5.3 %copy-start.1 = (f32[2,1,32,8,1024]{4,3,2,1,0:T(8,128)S(1)}, f32[2,1,32,8,1024]{4,3,2,1,0:T(8,128)}, u32[]{:S(2)}) copy-start(f32[2,1,32,8,1024]{4,3,2,1,0:T(8,128)} %param.19) | copy-start | bytes 6291460
  134.4 2.2 %copy-start.2 = (f32[1024,1024]{1,0:T(8,128)S(1)}, f32[1024,1024]{1,0:T(8,128)}, u32[]{:S(2)}) copy-start(f32[1024,1024]{1,0:T(8,128)} %param.22) | copy-start | bytes 12582916
  136.6 3.7 %copy-start.4 = (f32[1,32,8,1024]{3,2,1,0:T(8,128)S(1)}, f32[1,32,8,1024]{3,2,1,0:T(8,128)}, u32[]{:S(2)}) copy-start(f32[1,32,8,1024]{3,2,1,0:T(8,128)} %param.21) | copy-start | bytes 3145732

commit v5 on v3

--- a/solution.py
+++ b/solution.py
@@ -216,7 +216,10 @@
         copy.start()
     pl.semaphore_wait(barrier, devices - 1)
 
-    steps = sorted(range(1, devices), key=lambda step: abs(step - devices // 2))
+    ranked = sorted(range(1, devices), key=lambda step: abs(step - devices // 2))
+    middle = len(ranked) // 2
+    steps = [step for pair in zip(ranked[:middle], ranked[::-1]) for step in pair]
+    steps = steps + [step for step in ranked if step not in steps]
     copies = []
     for step in steps:
         peer = lax.rem(me + step, devices)

time: 137 us -> 137 us (level)
  no operation moved by 1% of the time
where the time goes in v5:
time: 137 us
  Pallas kernels  56.7 us (41%)
  waiting for transfers between devices  36.9 us (27%)
  matrix products  18.7 us (14%)
  local copies, waits for them, and re-layouts  8.96 us (7%)
  other arithmetic  7.09 us (5%)
  starting transfers between devices  5.35 us (4%)
  between operations  2.79 us (2%)
    pallas_call x1, Pallas kernels, spread(): pl.pallas_call(functools.partial(spread_kernel, devices), in_specs=[pl.Bl...  51.6 us
    all_to_all x1, waiting for transfers between devices, local_blocks(): back = lax.all_to_all(back, 'slab', split_axis=0, concat_axis=0, tiled=True)  36.9 us
    all_to_all x1, starting transfers between devices, local_blocks(): back = lax.all_to_all(back, 'slab', split_axis=0, concat_axis=0, tiled=True)  5.35 us
    pallas_call x1, Pallas kernels, finish(): pl.pallas_call(finish_kernel, grid=(blocks, parts), in_specs=[pl.BlockSpe...  5.09 us
    dot_general x1, matrix products, local_blocks(): surface = jnp.einsum('qpc,qca->qpa', stencil, field, precision=high_prec)  4.84 us
    add x1, local copies, waits for them, and re-layouts, local_blocks(): kinetic_bond[:, None, :, None]  4.18 us
    dot_general x1, matrix products, local_blocks(): jnp.einsum('kcb,ba->kca', wave, angular_dvr, precision=high_prec)  3.73 us
    dot_general x1, matrix products, local_blocks(): jnp.einsum('kca,ba->kcb', potential.reshape(1, cells, angles) * grid_wave...  3.72 us
  transfers between devices with their start and end apart: 1, of which 1 were waited for; matrix products, arithmetic and copies ran while one was open for 14% of the time, Pallas kernels for 0%

profile of v5, /device:TPU:13, one launch (start us, length us, event | category | flops | bytes accessed | tf_op | source)
XLA Modules:
  0.0 136.5 jit_solution(13951320349021214939)
XLA Ops:
  1.3 0.7 select_bitcast_fusion
  2.0 0.1 pad.9.clone
  2.1 0.7 fusion.36
  2.8 0.7 maximum_maximum_fusion.table_ref
  3.5 51.6 %shard_map.194 = (f32[16,256,128]{2,1,0:T(8,128)}, f32[16,8,128]{2,1,0:T(8,128)}) custom-call(f32[2,256,1024]{2,1,0:T(8,128)} %bitcast.60, f32[8,128]{1,0:T(8,128)} %maximum_maximum_fusion.table_ref), custom_call_target="tpu_custom_call" | custom-call | tf_op jit(solution)/shard_map/pallas_call | solution.py:260
  55.1 1.1 fusion.41
  56.2 4.8 %fusion.11 = f32[16,128,128]{2,1,0:T(8,128)S(1)} fusion(f32[16,256,128]{2,1,0:T(8,128)} %get-tuple-element.6, f32[16,128]{1,0:T(8,128)S(1)} %bitcast.69, f32[16,128]{1,0:T(8,128)S(1)} %get-tuple-element.25, f32[16,128]{1,0:T(8,128)S(1)} %bitcast.70, f32[16,128]{1,0:T(8,128)S(1)} %get-tuple-element.26, f32[16,128]{1,0:T(8,128)S(1)} %bitcast.71, ...), kind=kOutput, calls=%fused_computation.16 | convolution fusion | flops 408420352 | bytes 3211264 | tf_op jit(solution)/shard_map/qpc,qca->qpa/dot_general | solution.py:320
  61.1 0.2 reduce-precision_convert_fusion
  61.3 1.4 %fusion = f32[1024,256]{1,0:T(8,128)S(1)} fusion(f32[2048]{0:T(1024)S(1)} %bitcast.67, bf16[2048,128]{1,0:T(8,128)(2,1)S(1)} %get-tuple-element.17, bf16[2048,128]{1,0:T(8,128)(2,1)S(1)} %get-tuple-element.16), kind=kOutput, calls=%fused_computation.1 | convolution fusion | flops 1077936128 | bytes 2105344 | tf_op jit(solution)/shard_map/dot_general | solution.py:150
  62.7 0.1 copy-done.3
  62.9 2.0 %fusion.8 = f32[256,128,16]{1,2,0:T(8,128)S(1)} fusion(f32[16,256,128]{2,1,0:T(8,128)S(1)} %copy-done.3, f32[16,16]{1,0:T(8,128)S(1)} %copy-done), kind=kOutput, calls=%fused_computation.13 | convolution fusion | flops 50331648 | bytes 4195328 | tf_op jit(solution)/shard_map/ij,jca->ica/dot_general | solution.py:314
  64.9 0.7 copy.33
  65.6 1.8 %pad_maximum_fusion = f32[16,320,128]{2,1,0:T(8,128)} fusion(f32[16,64,128]{2,1,0:T(8,128)S(1)} %bitcast.62, f32[16,256,128]{2,1,0:T(8,128)S(1)} %bitcast.61), kind=kLoop, calls=%fused_computation.8 | loop fusion | flops 655360 | bytes 5242880 | tf_op jit(solution)/shard_map/concatenate | solution.py:324
  67.3 5.4 %all-to-all-start = ((f32[16,320,128]{2,1,0:T(8,128)}), f32[16,320,128]{2,1,0:T(8,128)}, u32[]{:S(2)}, u32[]{:S(2)}) async-start(f32[16,320,128]{2,1,0:T(8,128)} %pad_maximum_fusion), calls=%async_computation | async-start | bytes 5242880 | tf_op jit(solution)/shard_map/all_to_all | solution.py:325
  74.0 2.7 %multiply_add_fusion = f32[32,8,32,8]{3,2,1,0:T(8,128)} fusion(f32[8,8]{1,0:T(8,128)S(1)} %copy-done.9, f32[32,32]{1,0:T(8,128)S(1)} %fusion.33, f32[8,8]{1,0:T(8,128)S(1)} %fusion.35, f32[32,32]{1,0:T(8,128)S(1)} %copy-done.5), kind=kLoop, calls=%fused_computation.6 | loop fusion | flops 196608 | bytes 270848 | tf_op jit(solution)/shard_map/add | solution.py:328
  76.7 4.2 %reshape.187 = f32[256,256,1]{1,0,2:T(8,128)S(1)} reshape(f32[32,8,32,8]{3,2,1,0:T(8,128)} %multiply_add_fusion) | data formatting | bytes 524288 | tf_op jit(solution)/shard_map/add | solution.py:328
  81.0 0.7 reshape.190.damp_ref
  81.8 0.3 multiply_bitcast_fusion.1
  82.1 1.9 %copy-done.2 = f32[1024,1024]{1,0:T(8,128)S(1)} copy-done((f32[1024,1024]{1,0:T(8,128)S(1)}, f32[1024,1024]{1,0:T(8,128)}, u32[]{:S(2)}) %copy-start.2) | copy-done | bytes 4194328
  84.0 3.7 %fusion.3 = f32[2,256,1024]{2,1,0:T(8,128)S(1)} fusion(f32[1024,1024]{1,0:T(8,128)S(1)} %copy-done.2, f32[2,1,32,8,1024]{4,3,2,1,0:T(8,128)S(1)} %copy-done.1), kind=kOutput, calls=%fused_computation.4 | convolution fusion | flops 3221225472 | bytes 8388608 | tf_op jit(solution)/shard_map/kcb,ba->kca/dot_general | solution.py:332
  87.8 3.7 %fusion.1 = f32[2,256,1024]{2,1,0:T(8,128)S(1)} fusion(f32[1024,1024]{1,0:T(8,128)S(1)} %copy-done.2, f32[2,256,1024]{2,1,0:T(8,128)S(1)} %fusion.3, f32[256,1024]{1,0:T(8,128)S(1)} %bitcast.64), kind=kOutput, calls=%fused_computation.2 | convolution fusion | flops 3221749760 | bytes 9437184 | tf_op jit(solution)/shard_map/kca,ba->kcb/dot_general | solution.py:333
  91.5 3.0 %fusion.7.own_ref = f32[2,256,1024]{2,1,0:T(8,128)} fusion(f32[2,256,1024]{2,1,0:T(8,128)S(1)} %fusion.1, f32[1,256,1024]{2,1,0:T(8,128)S(1)} %get-tuple-element.15, f32[1,256,1024]{2,1,0:T(8,128)S(1)} %get-tuple-element.14, f32[256,256,1]{1,0,2:T(8,128)S(1)} %reshape.187, f32[1024]{0:T(1024)S(1)} %broadcast_multiply_fusion, ...), kind=kOutput, calls=%fused_computation.11 | convolution fusion | flops 808452096 | bytes 8663040 | tf_op jit(solution)/shard_map/cd,kda->kca/dot_general | solution.py:331
  94.5 36.9 %all-to-all-done.back_ref = f32[16,320,128]{2,1,0:T(8,128)} async-done(((f32[16,320,128]{2,1,0:T(8,128)}), f32[16,320,128]{2,1,0:T(8,128)}, u32[]{:S(2)}, u32[]{:S(2)}) %all-to-all-start) | async-done | bytes 2621472 | tf_op jit(solution)/shard_map/all_to_all | solution.py:325
  131.4 5.1 %shard_map.195 = (f32[2,256,1024]{2,1,0:T(8,128)}, f32[2,64,1024]{2,1,0:T(8,128)}) custom-call(f32[16,320,128]{2,1,0:T(8,128)} %all-to-all-done.back_ref, f32[2,256,1024]{2,1,0:T(8,128)} %fusion.7.own_ref, f32[2,256,1024]{2,1,0:T(8,128)} %bitcast.63, f32[256,1]{1,0:T(8,128)} %reshape.190.damp_ref), custom_call_target="tpu_custom_call" | custom-call | tf_op jit(solution)/shard_map/pallas_call | solution.py:173
  (29 shorter events, 0.3 us)
Async XLA Ops:
  0.6 62.1 %copy-start = (f32[16,16]{1,0:T(8,128)S(1)}, f32[16,16]{1,0:T(8,128)}, u32[]{:S(2)}) copy-start(f32[16,16]{1,0:T(8,128)} %param.23) | copy-start | bytes 3076
  61.3 1.6 %copy-start.3 = (f32[16,256,128]{2,1,0:T(8,128)S(1)}, f32[16,256,128]{2,1,0:T(8,128)}, u32[]{:S(2)}) copy-start(f32[16,256,128]{2,1,0:T(8,128)} %get-tuple-element.6) | copy-start | bytes 6291460
  67.3 6.7 %copy-start.5 = (f32[32,32]{1,0:T(8,128)S(1)}, f32[32,32]{1,0:T(8,128)}, u32[]{:S(2)}) copy-start(f32[32,32]{1,0:T(8,128)} %param.24) | copy-start | bytes 12292
  67.3 6.7 %copy-start.9 = (f32[8,8]{1,0:T(8,128)S(1)}, f32[8,8]{1,0:T(8,128)}, u32[]{:S(2)}) copy-start(f32[8,8]{1,0:T(8,128)} %param.25) | copy-start | bytes 772
  67.3 64.1 %all-to-all-start = ((f32[16,320,128]{2,1,0:T(8,128)}), f32[16,320,128]{2,1,0:T(8,128)}, u32[]{:S(2)}, u32[]{:S(2)}) async-start(f32[16,320,128]{2,1,0:T(8,128)} %pad_maximum_fusion), calls=%async_computation | async-start | bytes 5242880 | tf_op jit(solution)/shard_map/all_to_all | solution.py:325
  76.7 4.2 %copy-start.6 = (f32[1,32,8]{1,2,0:T(8,128)S(1)}, f32[1,32,8]{1,2,0:T(8,128)}, u32[]{:S(2)}) copy-start(f32[1,32,8]{1,2,0:T(8,128)} %param.31) | copy-start | bytes 3076
  76.7 5.0 %copy-start.7 = (f32[1024]{0:T(1024)S(1)}, f32[1024]{0:T(1024)}, u32[]{:S(2)}) copy-start(f32[1024]{0:T(1024)} %param.30) | copy-start | bytes 12292
  76.7 5.0 %copy-start.8 = (f32[1024]{0:T(1024)S(1)}, f32[1024]{0:T(1024)}, u32[]{:S(2)}) copy-start(f32[1024]{0:T(1024)} %param.27) | copy-start | bytes 12292
  76.7 5.0 %copy-start.10 = (f32[2]{0:T(128)S(1)}, f32[2]{0:T(128)}, u32[]{:S(2)}) copy-start(f32[2]{0:T(128)} %param.28) | copy-start | bytes 28
  76.7 5.1 %copy-start.1 = (f32[2,1,32,8,1024]{4,3,2,1,0:T(8,128)S(1)}, f32[2,1,32,8,1024]{4,3,2,1,0:T(8,128)}, u32[]{:S(2)}) copy-start(f32[2,1,32,8,1024]{4,3,2,1,0:T(8,128)} %param.19) | copy-start | bytes 6291460
  81.8 2.2 %copy-start.2 = (f32[1024,1024]{1,0:T(8,128)S(1)}, f32[1024,1024]{1,0:T(8,128)}, u32[]{:S(2)}) copy-start(f32[1024,1024]{1,0:T(8,128)} %param.22) | copy-start | bytes 12582916
  84.0 3.7 %copy-start.4 = (f32[1,32,8,1024]{3,2,1,0:T(8,128)S(1)}, f32[1,32,8,1024]{3,2,1,0:T(8,128)}, u32[]{:S(2)}) copy-start(f32[1,32,8,1024]{3,2,1,0:T(8,128)} %param.21) | copy-start | bytes 3145732
